TPU v7x, 32 devices: a whole 2x2x4 slice. The times are simulated.
32 devices in a mesh: seg: 4 (over y, core), tm: 8 (over z, x).
Axes of the slice: x: 2, y: 2, z: 4, core: 2. Of those that a mesh axis runs over, the one named last changes fastest.
Arguments:
- transition: bfloat16 [64, 512, 512], P(('seg', 'tm')), may hold values from -1 to 1
- obs_gain: bfloat16 [64, 512, 512], P(('seg', 'tm')), may hold values from -0.0625 to 0.0625
- observed: bfloat16 [64, 4, 512], P(('seg', 'tm')), may hold values from -6 to 6
- init_mean: float32 [4, 512], replicated, may hold values from -6 to 6
- init_factor: float32 [512, 512], P('tm'), may hold values from -6 to 6
Outputs:
- means: float32 [64, 4, 512], P(('seg', 'tm'))
- factor_ends: float32 [4, 512, 512], P('seg', 'tm')
All inputs are finite; a program needn't handle non-finite values.
Results may differ from a plain program's by a relative error of at most 0.0003.
Values sent between devices are 32-bit elements; how exact they have to be, the bound alone decides.
No kernel may reach another device: no remote copies, remote signals or barrier semaphores. Data moves between devices by JAX's collectives and lax.ppermute only.
A program may use at most 128 MiB of HBM per device.

v0:
```python
import jax
import jax.numpy as jnp
from jax import lax
from jax.experimental import pallas as pl
from jax.experimental.pallas import tpu as pltpu
from jax.sharding import PartitionSpec as P

F32 = jnp.float32
BF16 = jnp.bfloat16
AXES = ("seg", "tm")
GRANT = 10 * 1024 * 1024


def halves(x):
    hi = x.astype(BF16)
    return hi, (x - hi.astype(F32)).astype(BF16)


def dot(a, b):
    return jnp.dot(a, b, preferred_element_type=F32)


def dot3(a_hi, a_lo, b_hi, b_lo):
    return dot(a_hi, b_hi) + (dot(a_hi, b_lo) + dot(a_lo, b_hi))


def few(rows, hi, lo=None):
    r_hi = rows.astype(BF16)
    r_hi32 = r_hi.astype(F32)
    both = jnp.concatenate([r_hi32, rows - r_hi32]).astype(BF16)
    res = dot(both, hi)
    res = res[: rows.shape[0]] + res[rows.shape[0] :]
    return res if lo is None else res + dot(r_hi, lo)


class Sizes:
    def __init__(self, width, series, chunks):
        self.width, self.series, self.chunks = width, series, chunks
        self.part = width // chunks
        self.tall = width + 16 * (-(-series // 16))
        self.buf = width + 8 * (-(-chunks * series // 8))
        self.low = self.tall - width


def put_rows(z, out, body, tail):
    for j in range(z.chunks):
        cols = slice(j * z.part, (j + 1) * z.part)
        out[j * z.part : (j + 1) * z.part, :] = body[:, cols]
        out[z.width + j * z.series : z.width + (j + 1) * z.series, :] = tail[:, cols]


def put_cols(z, out, body, tail):
    out[: z.width, :] = body
    out[z.width : z.width + z.series, :] = tail


def gather_rows(z, bufs, full):
    for k, buf in enumerate(bufs):
        for j in range(z.chunks):
            full[k * z.part : (k + 1) * z.part, j * z.part : (j + 1) * z.part] = buf[j * z.part : (j + 1) * z.part, :]
    for j in range(z.chunks):
        full[z.width : z.width + z.series, j * z.part : (j + 1) * z.part] = bufs[0][
            z.width + j * z.series : z.width + (j + 1) * z.series, :
        ]


def gather_cols(z, bufs, full):
    for k, buf in enumerate(bufs):
        cols = slice(k * z.part, (k + 1) * z.part)
        full[: z.width, cols] = buf[: z.width, :]
        full[z.width : z.width + z.series, cols] = buf[z.width : z.width + z.series, :]


def clear_low(z, full):
    full[z.width :, :] = jnp.zeros((z.low, z.width), F32)


def put_chunks(z, by_rows, outs, full):
    @pl.when(by_rows)
    def _():
        for k, out in enumerate(outs):
            put_rows(z, out, full[k * z.part : (k + 1) * z.part, :], full[z.width : z.width + z.series, :])

    @pl.when(jnp.logical_not(by_rows))
    def _():
        for k, out in enumerate(outs):
            cols = slice(k * z.part, (k + 1) * z.part)
            put_cols(z, out, full[: z.width, cols], full[z.width : z.width + z.series, cols])


def call(kernel, outs, operands, where=None, scratch=(), far=0):
    in_specs = [pl.BlockSpec(memory_space=pltpu.HBM if i < far else pltpu.VMEM) for i in range(len(operands))]
    operands = [pltpu.with_memory_space_constraint(x, pltpu.HBM) if i < far else x for i, x in enumerate(operands)]

    def body(*refs):
        if where is None:
            kernel(*refs)
        else:
            kernel(where(lax.axis_index("seg"), lax.axis_index("tm")), *refs)

    return pl.pallas_call(
        body,
        out_shape=outs,
        in_specs=in_specs,
        out_specs=jax.tree.map(lambda _: pl.BlockSpec(memory_space=pltpu.VMEM), outs),
        scratch_shapes=list(scratch),
        compiler_params=pltpu.CompilerParams(vmem_limit_bytes=GRANT),
    )(*operands)


def shape(rows, cols, dtype=F32):
    return jax.ShapeDtypeStruct((rows, cols), dtype)


def gather(z, by_rows, bufs, full):
    @pl.when(by_rows)
    def _():
        gather_rows(z, bufs, full)

    @pl.when(jnp.logical_not(by_rows))
    def _():
        gather_cols(z, bufs, full)


def map_shapes(z):
    return [shape(z.tall, z.width, BF16), shape(z.tall, z.width, BF16), shape(z.series, z.width)]


def local_map(z, where, transition, gain, observed, sender):
    steps = transition.shape[0]
    count = z.chunks if sender else 4

    def kernel(flag, *refs):
        by_rows, active = flag
        pl.when(active)(lambda: run(by_rows, *refs))

    def run(by_rows, t_hbm, g_hbm, o_hbm, *rest):
        outs, drive, t, g, o, sems = rest[:count], *rest[count : count + 5]
        whole = rest[-1] if sender else outs[0]
        copies = [
            pltpu.make_async_copy(t_hbm, t, sems.at[0]),
            pltpu.make_async_copy(g_hbm, g, sems.at[1]),
            pltpu.make_async_copy(o_hbm, o, sems.at[2]),
        ]
        for copy in copies:
            copy.start()
        copies[0].wait()
        body = t[0]
        for i in range(1, steps):
            if i == 1:
                body = dot(body, t[i])
            else:
                b_hi, b_lo = halves(body)
                body = dot(b_hi, t[i]) + dot(b_lo, t[i])
        clear_low(z, whole)
        whole[: z.width, :] = body.astype(F32)
        copies[1].wait()
        copies[2].wait()
        drives = [dot(o[i], g[i]) for i in range(steps)]
        low = drives[0]
        for i in range(steps):
            drive[i] = drives[i]
            if i:
                l_hi, l_lo = halves(low)
                low = dot(l_hi, t[i]) + dot(l_lo, t[i]) + drives[i]
        whole[z.width : z.width + z.series, :] = low
        if sender:
            put_chunks(z, by_rows, outs, whole)
        else:
            _, hi, lo, tail = outs
            tail[...] = low
            hi[...], lo[...] = halves(whole[...])

    shapes = [shape(z.buf, z.part)] * z.chunks if sender else [shape(z.tall, z.width), *map_shapes(z)]
    res = call(
        kernel,
        shapes + [jax.ShapeDtypeStruct((steps, z.series, z.width), F32)],
        [transition, gain, observed],
        where,
        scratch=[
            pltpu.VMEM(transition.shape, transition.dtype),
            pltpu.VMEM(gain.shape, gain.dtype),
            pltpu.VMEM(observed.shape, observed.dtype),
            pltpu.SemaphoreType.DMA((3,)),
        ]
        + ([pltpu.VMEM((z.tall, z.width), F32)] if sender else []),
        far=3,
    )
    return (res[:-1], res[-1]) if sender else (res[0], tuple(res[1:4]), res[-1])


def quarter(z, ref, k):
    return ref.at[pl.ds(k * z.buf, z.buf)]


def split_parts(z, refs):
    return [quarter(z, ref, k) for ref in refs for k in range(ref.shape[0] // z.buf)]


def times_chunk(z, where, chunk, own):
    count = chunk.shape[0] // z.buf
    span = count * z.part

    def kernel(by_rows, got, own_hi, own_lo, own_tail, *rest):
        outs, (left, right) = rest[:count], rest[count:]
        gots = split_parts(z, [got])

        @pl.when(by_rows)
        def _():
            left[span:, :] = jnp.zeros((left.shape[0] - span, z.width), F32)
            for j in range(z.chunks):
                cols = slice(j * z.part, (j + 1) * z.part)
                for q, part in enumerate(gots):
                    left[q * z.part : (q + 1) * z.part, cols] = part[j * z.part : (j + 1) * z.part, :]
                left[span : span + z.series, cols] = gots[0][z.width + j * z.series : z.width + (j + 1) * z.series, :]
            l_hi, l_lo = halves(left[...])
            res = dot3(l_hi, l_lo, own_hi[: z.width, :], own_lo[: z.width, :])
            for q, out in enumerate(outs):
                put_rows(z, out, res[q * z.part : (q + 1) * z.part], res[span : span + z.series] + own_tail[...])

        @pl.when(jnp.logical_not(by_rows))
        def _():
            for q, part in enumerate(gots):
                right[:, q * z.part : (q + 1) * z.part] = part[: z.width + z.series, :]
            r_hi, r_lo = halves(right[: z.width, :])
            res = dot3(own_hi[...], own_lo[...], r_hi, r_lo)
            low = res[z.width : z.width + z.series] + right[z.width : z.width + z.series, :]
            for q, out in enumerate(outs):
                cols = slice(q * z.part, (q + 1) * z.part)
                out[z.width :, :] = jnp.zeros((z.buf - z.width, z.part), F32)
                put_cols(z, out, res[: z.width, cols], low[:, cols])

    return call(
        kernel,
        [shape(z.buf, z.part)] * count,
        [chunk, *own],
        where,
        scratch=[pltpu.VMEM((span + z.low, z.width), F32), pltpu.VMEM((z.width + z.series, span), F32)],
    )


def merge(z, where, got, own):
    sent = z.chunks

    def kernel(flag, *refs):
        by_rows, got_left, next_rows = flag
        n = z.chunks
        gots, owns = refs[:n], refs[n : 2 * n]
        outs = split_parts(z, refs[2 * n : 2 * n + sent])
        hi, lo, tail, left_hi, left_lo, left_tail = refs[2 * n + sent : 2 * n + sent + 6]
        a, b, c = refs[2 * n + sent + 6 :]
        clear_low(z, a)
        clear_low(z, b)

        @pl.when(got_left)
        def _():
            gather(z, by_rows, gots, a)
            gather(z, by_rows, owns, b)

        @pl.when(jnp.logical_not(got_left))
        def _():
            gather(z, by_rows, owns, a)
            gather(z, by_rows, gots, b)

        left_hi[...], left_lo[...] = halves(a[...])
        left_tail[...] = a[z.width : z.width + z.series, :]
        r_hi, r_lo = halves(b[: z.width, :])
        c[...] = dot3(left_hi[...], left_lo[...], r_hi, r_lo)
        c[z.width : z.width + z.series, :] = c[z.width : z.width + z.series, :] + b[z.width : z.width + z.series, :]
        put_chunks(z, next_rows, outs, c)
        hi[...], lo[...] = halves(c[...])
        tail[...] = c[z.width : z.width + z.series, :]

    res = call(
        kernel,
        [shape(z.chunks // sent * z.buf, z.part)] * sent + map_shapes(z) * 2,
        list(got) + list(own),
        where,
        scratch=[pltpu.VMEM((z.tall, z.width), F32)] * 3,
    )
    return res[:sent], tuple(res[sent : sent + 3]), tuple(res[sent + 3 :])


def merge_first(z, where, got, own, count):
    span = z.width // count
    n = z.chunks

    def kernel(flag, *refs):
        by_rows, got_left, next_rows = flag
        gots, owns = refs[:n], refs[n : 2 * n]
        out, left_hi, left_lo, left_tail, right_hi, right_lo, right_tail, a, b, c = refs[2 * n :]
        outs = split_parts(z, [out])
        clear_low(z, a)
        clear_low(z, b)

        @pl.when(got_left)
        def _():
            gather(z, by_rows, gots, a)
            gather(z, by_rows, owns, b)

        @pl.when(jnp.logical_not(got_left))
        def _():
            gather(z, by_rows, owns, a)
            gather(z, by_rows, gots, b)

        left_hi[...], left_lo[...] = halves(a[...])
        left_tail[...] = a[z.width : z.width + z.series, :]
        right_hi[...], right_lo[...] = halves(b[...])
        tail = b[z.width : z.width + z.series, :]
        right_tail[...] = tail

        @pl.when(next_rows)
        def _():
            c[:span, :] = a[:span, :]
            c[span : span + z.low, :] = a[z.width :, :]
            c_hi, c_lo = halves(c[: span + z.low, :])
            res = dot3(c_hi, c_lo, right_hi[: z.width, :], right_lo[: z.width, :])
            for q, part in enumerate(outs):
                put_rows(z, part, res[q * z.part : (q + 1) * z.part], res[span : span + z.series] + tail)

        @pl.when(jnp.logical_not(next_rows))
        def _():
            res = dot3(left_hi[...], left_lo[...], right_hi[: z.width, :span], right_lo[: z.width, :span])
            for q, part in enumerate(outs):
                cols = slice(q * z.part, (q + 1) * z.part)
                put_cols(z, part, res[: z.width, cols], res[z.width : z.width + z.series, cols] + tail[:, cols])

    res = call(
        kernel,
        [shape(z.chunks // count * z.buf, z.part)] + map_shapes(z) * 2,
        list(got) + list(own),
        where,
        scratch=[pltpu.VMEM((z.tall, z.width), F32)] * 3,
    )
    return res[0], tuple(res[1:4]), tuple(res[4:7])


def merge_rest(z, where, sent, left, right, count):
    span = z.width // count

    def kernel(flag, *refs):
        next_rows = flag[2]
        done, left_hi, left_lo, _, right_hi, right_lo, right_tail = refs[:7]
        outs = split_parts(z, refs[7 : 6 + count])
        hi, lo, tail, c = refs[6 + count :]
        gather(z, next_rows, split_parts(z, [done]), c)

        @pl.when(next_rows)
        def _():
            c[span:, :] = dot3(left_hi[span:, :], left_lo[span:, :], right_hi[: z.width, :], right_lo[: z.width, :])
            low = c[z.width : z.width + z.series, :] + right_tail[...]
            c[z.width : z.width + z.series, :] = low
            for q, part in enumerate(outs):
                at = span + q * z.part
                put_rows(z, part, c[at : at + z.part, :], low)

        @pl.when(jnp.logical_not(next_rows))
        def _():
            c[z.width + z.series :, :span] = jnp.zeros((z.low - z.series, span), F32)
            c[:, span:] = dot3(left_hi[...], left_lo[...], right_hi[: z.width, span:], right_lo[: z.width, span:])
            low = c[z.width : z.width + z.series, span:] + right_tail[:, span:]
            c[z.width : z.width + z.series, span:] = low
            for q, part in enumerate(outs):
                cols = slice(span + q * z.part, span + (q + 1) * z.part)
                put_cols(z, part, c[: z.width, cols], low[:, q * z.part : (q + 1) * z.part])

        hi[...], lo[...] = halves(c[...])
        tail[...] = c[z.width : z.width + z.series, :]

    res = call(
        kernel,
        [shape(z.chunks // count * z.buf, z.part)] * (count - 1) + map_shapes(z),
        [sent, *left, *right],
        where,
        scratch=[pltpu.VMEM((z.tall, z.width), F32)],
    )
    return [sent, *res[: count - 1]], tuple(res[count - 1 :])


def assemble(z, where, chunks, others=None, with_tail=True):
    extra = [] if others is None else list(others)

    def kernel(flag, *refs):
        by_rows, swap = flag
        n = len(chunks)
        bufs, rest = split_parts(z, refs[:n]), refs[n : n + len(extra)]
        hi, lo, *tail, full = refs[n + len(extra) :]
        clear_low(z, full)
        if not extra:
            gather(z, by_rows, bufs, full)
        else:

            @pl.when(jnp.logical_not(swap))
            def _():
                gather(z, by_rows, bufs, full)

            @pl.when(swap)
            def _():
                if len(rest) == 1:
                    full[...] = rest[0][...]
                else:
                    gather(z, by_rows, rest, full)

        hi[...], lo[...] = halves(full[...])
        if with_tail:
            tail[0][...] = full[z.width : z.width + z.series, :]

    return call(
        kernel,
        map_shapes(z) if with_tail else map_shapes(z)[:2],
        list(chunks) + extra,
        where,
        scratch=[pltpu.VMEM((z.tall, z.width), F32)],
    )


def padded(series):
    return 8 * (-(-series // 8))


def advance(z, where, parts, block, before=None, split=False):
    rows = sum(p.shape[0] for p in parts)
    operands = list(parts) + list(block[:2]) + ([] if before is None else [before])
    m = len(parts)

    def kernel(active, *refs):
        given, (hi, lo), outs = refs[:m], refs[m : m + 2], refs[len(operands) :]

        def put(value):
            for i, out in enumerate(outs):
                out[...] = value[i * out.shape[0] : (i + 1) * out.shape[0]]

        def run():
            state = given[0][...] if m == 1 else jnp.concatenate([g[...] for g in given])
            put(few(state, hi[: z.width, :], lo[: z.width, :]))

        pl.when(active)(run)
        if before is not None:

            @pl.when(jnp.logical_not(active))
            def _():
                put(refs[m + 2][...])

    outs = [shape(rows // 2, z.width)] * 2 if split else [shape(rows, z.width)]
    res = call(kernel, outs, operands, where)
    return res if split else res[0]


def advance_mean(z, mean, block):
    low = padded(z.series)

    def kernel(given, hi, lo, tail, out):
        now = given[...]
        if given.shape[0] < low:
            now = jnp.concatenate([now, jnp.zeros((low - given.shape[0], z.width), F32)])
        out[...] = few(now, hi[: z.width, :], lo[: z.width, :])
        out[: z.series, :] = out[: z.series, :] + tail[...]

    return call(kernel, shape(low, z.width), [mean, *block])


def deal(where, kept, got):
    def kernel(received, a, b, out):
        @pl.when(received)
        def _():
            out[0] = b[...]

        @pl.when(jnp.logical_not(received))
        def _():
            out[0] = a[...]

    return call(kernel, jax.ShapeDtypeStruct((1, *kept.shape), F32), [kept, got], where)


def load_choice(z, index, refs, into):
    for i, ref in enumerate(refs):

        @pl.when(index == i)
        def _():
            if ref.shape[0] == z.series:
                into[...] = jnp.zeros(into.shape, F32)
                into[: z.series, :] = ref[...]
            else:
                into[...] = ref[ref.shape[0] - into.shape[0] :, :]


def descend(z, where, candidates, left, cross=None):
    low = padded(z.series)
    m = len(candidates)
    maps = list(left) + ([] if cross is None else list(cross))

    def kernel(flag, *refs):
        index, through, in_right = flag
        hi, lo, tail = refs[m : m + 3]
        mine, other, now = refs[m + len(maps) :]
        load_choice(z, index, refs[:m], now)
        if cross is not None:

            @pl.when(through)
            def _():
                c_hi, c_lo, c_tail = refs[m + 3 : m + 6]
                now[...] = few(now[...], c_hi[: z.width, :], c_lo[: z.width, :])
                now[: z.series, :] = now[: z.series, :] + c_tail[...]

        beyond = few(now[...], hi[: z.width, :], lo[: z.width, :])

        @pl.when(in_right)
        def _():
            mine[...] = beyond
            mine[: z.series, :] = mine[: z.series, :] + tail[...]
            other[...] = now[...]

        @pl.when(jnp.logical_not(in_right))
        def _():
            other[...] = beyond
            other[: z.series, :] = other[: z.series, :] + tail[...]
            mine[...] = now[...]

    return call(
        kernel, [shape(low, z.width)] * 2, [*candidates, *maps], where, scratch=[pltpu.VMEM((low, z.width), F32)]
    )


def last_steps(z, where, candidates, left, transition, drives):
    steps = transition.shape[0]
    m = len(candidates)
    low = padded(z.series)

    def kernel(flag, *refs):
        index, through, second = flag
        hi, lo, tail, t, d0, d1, out, now = refs[m:]
        load_choice(z, index, refs[:m], now)

        @pl.when(through)
        def _():
            now[...] = few(now[...], hi[: z.width, :], lo[: z.width, :])
            now[: z.series, :] = now[: z.series, :] + tail[...]

        for i in range(steps):
            now[...] = few(now[...], t[i])
            now[: z.series, :] = now[: z.series, :] + jnp.where(second, d1[i], d0[i])
            out[i] = now[: z.series, :]

    return call(
        kernel,
        jax.ShapeDtypeStruct((steps, z.series, z.width), F32),
        [*candidates, *left, transition, *drives],
        where,
        scratch=[pltpu.VMEM((low, z.width), F32)],
    )


class Tree:
    def __init__(self, segs, size):
        self.segs, self.size = segs, size
        self.depth = size.bit_length() - 1
        if size != 1 << self.depth or self.depth < 3:
            raise ValueError("tm size")

    def root(self, odd, level, group):
        if level == 1:
            return 2 * group + (0 if odd else 1)
        return self.root(odd, level - 1, 2 * group + (1 - group % 2))

    def pairs(self, per_parity):
        return [
            (s * self.size + a, s * self.size + b) for s in range(self.segs) for a, b in per_parity(s % 2)
        ]

    def child_roots(self, odd, level, group):
        return self.root(odd, level - 1, 2 * group), self.root(odd, level - 1, 2 * group + 1)

    def up(self, level):
        def of(odd):
            if level == 1:
                return [(i, i ^ 1) for i in range(self.size) if i % 2 == (1 if odd else 0)]
            found = []
            for g in range(self.size >> level):
                a, b = self.child_roots(odd, level, g)
                if level == self.depth:
                    found += [(a, b), (b, a)]
                else:
                    found.append((a, b) if g % 2 == 0 else (b, a))
            return found

        return self.pairs(of)

    def far(self, bit, seg=None):
        found = []
        for s in range(self.segs) if seg is None else [seg]:
            for i in range(self.size):
                away = i // 2 ^ self.root(0, self.depth - 1, 2 * i // self.size) // 2
                if bit <= away < 2 * bit:
                    found.append((s * self.size + i, s * self.size + (i ^ 2 * bit)))
        return found

    def holds(self, i):
        return i // 2 == self.root(0, self.depth - 1, 2 * i // self.size) // 2

    def root_of(self, odd, level, group):
        for _ in range(level - 1):
            group = 2 * group + 1 - group % 2
        return 2 * group + 1 - odd


def tied(x, after):
    return lax.optimization_barrier((x, after))[0]


def make(mesh):
    segs, size = mesh.shape["seg"], mesh.shape["tm"]
    tree = Tree(segs, size)
    depth = tree.depth
    half = size // 2

    def send(x, pairs):
        return lax.ppermute(x, AXES, pairs)

    def others(level, flip):
        def of(odd):
            found = []
            for g in range(size >> level):
                root = tree.root(odd, level, g)
                a, b = tree.child_roots(odd, level, g)
                found.append((root, (a if root == b else b) ^ flip))
            return found

        return tree.pairs(of)

    def top_and_other(seg, tm, level):
        odd, group = seg % 2, tm >> level
        top = tree.root_of(odd, level, group)
        a, b = (tree.root_of(odd, level - 1, 2 * group + i) for i in (0, 1))
        return top, a + b - top

    def per_device(transition, obs_gain, observed, init_mean, init_factor):
        width, series = transition.shape[1], observed.shape[1]
        chunks = next(n for n in (4, 2, 1) if width % (n * 128) == 0 or n == 1)
        z = Sizes(width, series, chunks)

        def is_even(seg, tm):
            return seg % 2 == 0

        def in_right_half(seg, tm):
            return tm >= half

        def sends(seg, tm):
            return seg % 2 == 0, (seg + tm) % 2 == 0

        def receives(seg, tm):
            return seg % 2 == 0, (seg + tm) % 2 == 1

        def one_chunk(c):
            return times_chunk(z, is_even, c, own_map)[0]

        own, early = local_map(z, sends, transition, obs_gain, observed, True)
        first = [send(c, tree.up(1)) for c in own]
        whole, own_map, late = local_map(z, receives, transition, obs_gain, observed, False)
        outs = [one_chunk(c) for c in first]
        back = send(tied(whole, outs), tree.pairs(lambda odd: [(i, i + 1) for i in range(0, size, 2)] if odd else []))
        bits = [1 << i for i in range(depth - 3, -1, -1)]
        start = [init_factor]
        for bit in bits:
            held = start[0] if len(start) == 1 else jnp.concatenate(start)
            start = [held, send(tied(held, outs), tree.far(bit, 0))]
        lefts = {}
        for level in range(2, depth):

            def where(seg, tm, level=level):
                by_rows = seg % 2 == 0 if level == 2 else seg >= 0
                next_rows = tm < half if level == depth - 1 else seg >= 0
                return by_rows, (tm >> level) % 2 == 0, next_rows

            got = [send(c, tree.up(level)) for c in outs]
            if level < depth - 1 or chunks == 1:
                outs, mine, lefts[level] = merge(z, where, got, outs)
            else:
                sent, lefts[level], right = merge_first(z, where, got, outs, 2)
                outs, mine = merge_rest(z, where, sent, lefts[level], right, 2)
        crossed = [send(c, tree.up(depth)) for c in outs]
        final = [part for c in crossed for part in times_chunk(z, in_right_half, c, mine)]
        a, b = tree.child_roots(0, depth, 0)
        halved = send(advance_mean(z, init_mean, mine), [(a, b)])
        onward = advance_mean(z, halved, mine)
        nexts = [(b, size + r) for r in tree.child_roots(1, depth, 0)]
        second = send(onward, nexts[1:]) + send(onward, nexts[:1])
        roots = tree.pairs(lambda odd: [(r, r ^ 1) for r in tree.child_roots(odd, depth, 0)])
        got = [send(c, roots) for c in final]
        left = assemble(z, lambda seg, tm: (seg >= 0, seg % 2 == 1), first, [back])
        halfway = assemble(z, lambda seg, tm: (seg >= 0, seg < 0), crossed)
        got[-1], left, halfway = lax.optimization_barrier((got[-1], left, halfway))

        def beside(seg, tm):
            return tm >= half, tm ^ 1 == tree.root_of(seg % 2, depth - 1, tm // half)

        block = assemble(z, beside, final, got, with_tail=False)

        at_root = assemble(z, lambda seg, tm: (tm >= half, seg < 0), final)
        entries = [init_mean, second]
        for turn in range(2, segs):
            pairs = []
            for h in (0, 1):
                a, b = (tree.root(s % 2, depth - 1, h) for s in (turn - 1, turn))
                pairs.append(((turn - 1) * size + a, turn * size + b))
            gone = advance_mean(z, entries[-1], at_root)
            entries.append(send(gone, pairs))

        moved = advance(z, lambda seg, tm: seg == 0, start, block)
        for turn in range(1, segs):
            pairs = [((turn - 1) * size + i, turn * size + i) for i in range(size) if tree.holds(i)]
            arrived = send(moved, pairs)

            def where(seg, tm, turn=turn):
                return seg >= turn

            moved = advance(z, where, [arrived], block, moved, turn == segs - 1)

        def down(arrivals):
            candidates, cross = arrivals, halfway
            for level in range(depth - 1, 1, -1):

                def where(seg, tm, level=level):
                    if level == depth - 1:
                        index = seg
                    else:
                        index = (tm == top_and_other(seg, tm, level + 1)[1]).astype(jnp.int32)
                    return index, tm >= half, (tm >> level) % 2 == 0

                mine_in, other_in = descend(z, where, candidates, lefts[level], cross)
                candidates, cross = [mine_in, send(other_in, others(level, 0))], None
            near = tree.pairs(lambda odd: [(tree.root(odd, 2, g), tree.root(odd, 2, g) ^ 1) for g in range(size >> 2)])
            return [*candidates, send(other_in, others(2, 1)), send(mine_in, near)]

        candidates = down(entries)

        kept, given = moved
        for bit in reversed(bits):
            back_pairs = [(b, a) for a, b in tree.far(bit)]
            came = send(given, back_pairs)

            def where(seg, tm, bit=bit):
                away = tm // 2 ^ tree.root_of(0, depth - 1, tm // half) // 2
                return (away >= bit) & (away < 2 * bit)

            kept = deal(where, kept, came)
            if bit != bits[0]:
                rows = kept.shape[1] // 2
                kept, given = kept[0, :rows], kept[0, rows:]
        ends = kept

        def where(seg, tm):
            top, other = top_and_other(seg, tm, 2)
            index = jnp.where(tm == other, 1, jnp.where(tm == other ^ 1, 2, jnp.where(tm == top, 0, 3)))
            return index, tm % 2 == 1, (seg + tm) % 2 == 1

        return last_steps(z, where, candidates, left, transition, (early, late)), ends

    return per_device


def solution(mesh):
    return jax.shard_map(
        make(mesh),
        mesh=mesh,
        in_specs=(
            P(("seg", "tm"), None, None),
            P(("seg", "tm"), None, None),
            P(("seg", "tm"), None, None),
            P(),
            P("tm", None),
        ),
        out_specs=(P(("seg", "tm"), None, None), P("seg", "tm", None)),
        check_vma=False,
    )
```

profile of v0, /device:TPU:5, one launch (start us, length us, event | category | flops | bytes accessed | tf_op | source)
XLA Modules:
  0.0 100.3 jit_solution(18185752764995070682)
XLA Ops:
  0.7 1.3 %collective-permute-start.6 = (f32[528,128]{1,0:T(8,128)S(1)}, f32[528,128]{1,0:T(8,128)S(1)}, u32[]{:S(2)}, u32[]{:S(2)}) collective-permute-start(f32[528,128]{1,0:T(8,128)S(1)} %get-tuple-element.57), channel_id=1, source_target_pairs={{0,1},{2,3},{4,5},{6,7},{9,8},{11,10},{13,12},{15,14},{16,17},{18,... | collective-permute-start | bytes 811016 | tf_op jit(solution)/shard_map/ppermute | solution.py:617
  2.0 1.3 %collective-permute-start.4 = (f32[528,128]{1,0:T(8,128)S(1)}, f32[528,128]{1,0:T(8,128)S(1)}, u32[]{:S(2)}, u32[]{:S(2)}) collective-permute-start(f32[528,128]{1,0:T(8,128)S(1)} %get-tuple-element.56), channel_id=1, source_target_pairs={{0,1},{2,3},{4,5},{6,7},{9,8},{11,10},{13,12},{15,14},{16,17},{18,... | collective-permute-start | bytes 811016 | tf_op jit(solution)/shard_map/ppermute | solution.py:617
  3.3 1.3 %collective-permute-start.2 = (f32[528,128]{1,0:T(8,128)S(1)}, f32[528,128]{1,0:T(8,128)S(1)}, u32[]{:S(2)}, u32[]{:S(2)}) collective-permute-start(f32[528,128]{1,0:T(8,128)S(1)} %get-tuple-element.55), channel_id=1, source_target_pairs={{0,1},{2,3},{4,5},{6,7},{9,8},{11,10},{13,12},{15,14},{16,17},{18,... | collective-permute-start | bytes 811016 | tf_op jit(solution)/shard_map/ppermute | solution.py:617
  4.6 1.3 %collective-permute-start = (f32[528,128]{1,0:T(8,128)S(1)}, f32[528,128]{1,0:T(8,128)S(1)}, u32[]{:S(2)}, u32[]{:S(2)}) collective-permute-start(f32[528,128]{1,0:T(8,128)S(1)} %get-tuple-element.51), channel_id=1, source_target_pairs={{0,1},{2,3},{4,5},{6,7},{9,8},{11,10},{13,12},{15,14},{16,17},{18,... | collective-permute-start | bytes 811016 | tf_op jit(solution)/shard_map/ppermute | solution.py:617
  5.9 2.4 %shard_map.69 = (f32[528,512]{1,0:T(8,128)S(1)}, bf16[528,512]{1,0:T(8,128)(2,1)S(1)}, bf16[528,512]{1,0:T(8,128)(2,1)S(1)}, f32[4,512]{1,0:T(4,128)S(1)}, f32[2,4,512]{2,1,0:T(4,128)S(1)}) custom-call(bf16[2,512,512]{2,1,0:T(8,128)(2,1)} %refs_7_.1, bf16[2,512,512]{2,1,0:T(8,128)(2,1)} %refs_1_.3, bf16[2,4,512]{2,1,0:T(4,128)(2,1)} %refs_2_.3), custom_call_target="tpu_custom_call" | custom-call | tf_op jit(solution)/shard_map/pallas_call | solution.py:101
  8.3 0.9 collective-permute-done.6.refs_0_.refs_3_
  9.8 2.3 %collective-permute-done.4.refs_0_.refs_2_ = f32[528,128]{1,0:T(8,128)S(1)} collective-permute-done((f32[528,128]{1,0:T(8,128)S(1)}, f32[528,128]{1,0:T(8,128)S(1)}, u32[]{:S(2)}, u32[]{:S(2)}) %collective-permute-start.4) | collective-permute-done | bytes 270368 | tf_op jit(solution)/shard_map/ppermute | solution.py:617
  12.7 2.3 %collective-permute-done.2.refs_0_.refs_1_ = f32[528,128]{1,0:T(8,128)S(1)} collective-permute-done((f32[528,128]{1,0:T(8,128)S(1)}, f32[528,128]{1,0:T(8,128)S(1)}, u32[]{:S(2)}, u32[]{:S(2)}) %collective-permute-start.2) | collective-permute-done | bytes 270368 | tf_op jit(solution)/shard_map/ppermute | solution.py:617
  15.5 2.3 %collective-permute-done.refs_0_ = f32[528,128]{1,0:T(8,128)S(1)} collective-permute-done((f32[528,128]{1,0:T(8,128)S(1)}, f32[528,128]{1,0:T(8,128)S(1)}, u32[]{:S(2)}, u32[]{:S(2)}) %collective-permute-start) | collective-permute-done | bytes 270368 | tf_op jit(solution)/shard_map/ppermute | solution.py:617
  18.4 1.5 %collective-permute-start.16 = (f32[528,512]{1,0:T(8,128)S(1)}, f32[528,512]{1,0:T(8,128)S(1)}, u32[]{:S(2)}, u32[]{:S(2)}) collective-permute-start(f32[528,512]{1,0:T(8,128)S(1)} %get-tuple-element.77), channel_id=1, source_target_pairs={{8,9},{10,11},{12,13},{14,15},{24,25},{26,27},{28,29},{30,31}} | collective-permute-start | bytes 3244040 | tf_op jit(solution)/shard_map/ppermute | solution.py:617
  20.0 3.2 %collective-permute-start.1 = (f32[528,128]{1,0:T(8,128)S(1)}, f32[528,128]{1,0:T(8,128)S(1)}, u32[]{:S(2)}, u32[]{:S(2)}) collective-permute-start(f32[528,128]{1,0:T(8,128)S(1)} %shard_map.70.refs_4_), channel_id=1, source_target_pairs={{1,3},{7,5},{8,10},{14,12},{17,19},{23,21},{24,26},{30,28}} | collective-permute-start | bytes 811016 | tf_op jit(solution)/shard_map/ppermute | solution.py:617
  23.2 1.3 %collective-permute-start.3 = (f32[528,128]{1,0:T(8,128)S(1)}, f32[528,128]{1,0:T(8,128)S(1)}, u32[]{:S(2)}, u32[]{:S(2)}) collective-permute-start(f32[528,128]{1,0:T(8,128)S(1)} %shard_map.71.refs_5_), channel_id=1, source_target_pairs={{1,3},{7,5},{8,10},{14,12},{17,19},{23,21},{24,26},{30,28}} | collective-permute-start | bytes 811016 | tf_op jit(solution)/shard_map/ppermute | solution.py:617
  24.5 1.3 %collective-permute-start.5 = (f32[528,128]{1,0:T(8,128)S(1)}, f32[528,128]{1,0:T(8,128)S(1)}, u32[]{:S(2)}, u32[]{:S(2)}) collective-permute-start(f32[528,128]{1,0:T(8,128)S(1)} %shard_map.72.refs_6_), channel_id=1, source_target_pairs={{1,3},{7,5},{8,10},{14,12},{17,19},{23,21},{24,26},{30,28}} | collective-permute-start | bytes 811016 | tf_op jit(solution)/shard_map/ppermute | solution.py:617
  25.8 1.3 %collective-permute-start.7 = (f32[528,128]{1,0:T(8,128)S(1)}, f32[528,128]{1,0:T(8,128)S(1)}, u32[]{:S(2)}, u32[]{:S(2)}) collective-permute-start(f32[528,128]{1,0:T(8,128)S(1)} %shard_map.73.refs_7_), channel_id=1, source_target_pairs={{1,3},{7,5},{8,10},{14,12},{17,19},{23,21},{24,26},{30,28}} | collective-permute-start | bytes 811016 | tf_op jit(solution)/shard_map/ppermute | solution.py:617
  27.2 2.3 %collective-permute-done.3.refs_1_ = f32[528,128]{1,0:T(8,128)S(1)} collective-permute-done((f32[528,128]{1,0:T(8,128)S(1)}, f32[528,128]{1,0:T(8,128)S(1)}, u32[]{:S(2)}, u32[]{:S(2)}) %collective-permute-start.3) | collective-permute-done | bytes 270368 | tf_op jit(solution)/shard_map/ppermute | solution.py:617
  29.5 2.9 %collective-permute-done.5.refs_2_ = f32[528,128]{1,0:T(8,128)S(1)} collective-permute-done((f32[528,128]{1,0:T(8,128)S(1)}, f32[528,128]{1,0:T(8,128)S(1)}, u32[]{:S(2)}, u32[]{:S(2)}) %collective-permute-start.5) | collective-permute-done | bytes 270368 | tf_op jit(solution)/shard_map/ppermute | solution.py:617
  32.4 2.9 %collective-permute-done.7.refs_3_ = f32[528,128]{1,0:T(8,128)S(1)} collective-permute-done((f32[528,128]{1,0:T(8,128)S(1)}, f32[528,128]{1,0:T(8,128)S(1)}, u32[]{:S(2)}, u32[]{:S(2)}) %collective-permute-start.7) | collective-permute-done | bytes 270368 | tf_op jit(solution)/shard_map/ppermute | solution.py:617
  35.3 1.2 %shard_map.74 = (f32[1056,128]{1,0:T(8,128)S(1)}, bf16[528,512]{1,0:T(8,128)(2,1)S(1)}, bf16[528,512]{1,0:T(8,128)(2,1)S(1)}, f32[4,512]{1,0:T(4,128)S(1)}, bf16...) custom-call(f32[528,128]{1,0:T(8,128)S(1)} %collective-permute-done.1.refs_0_, ...), custom_call_target="tpu_custom_call" | custom-call | tf_op jit(solution)/shard_map/pallas_call | solution.py:101
  36.5 0.8 shard_map.75
  37.3 0.7 collective-permute-start.12
  38.0 0.7 collective-permute-start.11
  39.3 0.8 collective-permute-start.15
  40.2 0.7 collective-permute-start.23
  41.5 0.7 collective-permute-start.21
  42.2 0.7 collective-permute-start.22
  45.5 0.7 collective-permute-start.25
  46.6 0.7 collective-permute-start.26
  47.7 1.3 %collective-permute-start.27 = (f32[64,512]{1,0:T(8,128)S(1)}, f32[64,512]{1,0:T(8,128)S(1)}, u32[]{:S(2)}, u32[]{:S(2)}) collective-permute-start(f32[64,512]{1,0:T(8,128)S(1)} %get-tuple-element.99), channel_id=1, source_target_pairs={{2,0},{3,1},{4,6},{5,7},{10,8},{11,9},{12,14},{13,15},{18,16},{19,... | collective-permute-start | bytes 393224 | tf_op jit(solution)/shard_map/ppermute | solution.py:617
  53.1 0.8 collective-permute-start.14
  55.5 1.3 %collective-permute-start.17 = (f32[8,512]{1,0:T(8,128)S(1)}, f32[8,512]{1,0:T(8,128)S(1)}, u32[]{:S(2)}, u32[]{:S(2)}) collective-permute-start(f32[8,512]{1,0:T(8,128)S(1)} %get-tuple-element.88), channel_id=1, source_target_pairs={{3,1},{5,7},{10,8},{12,14},{19,17},{21,23},{26,24},{28,30}} | collective-permute-start | bytes 49160 | tf_op jit(solution)/shard_map/ppermute | solution.py:617
  56.8 41.9 %collective-permute-done.17.refs_1_ = f32[8,512]{1,0:T(8,128)S(1)} collective-permute-done((f32[8,512]{1,0:T(8,128)S(1)}, f32[8,512]{1,0:T(8,128)S(1)}, u32[]{:S(2)}, u32[]{:S(2)}) %collective-permute-start.17) | collective-permute-done | bytes 16416 | tf_op jit(solution)/shard_map/ppermute | solution.py:617
  98.7 1.0 shard_map.86
  (56 shorter events, 13.2 us)
Async XLA Ops:
  0.7 8.5 %collective-permute-start.6 = (f32[528,128]{1,0:T(8,128)S(1)}, f32[528,128]{1,0:T(8,128)S(1)}, u32[]{:S(2)}, u32[]{:S(2)}) collective-permute-start(f32[528,128]{1,0:T(8,128)S(1)} %get-tuple-element.57), channel_id=1, source_target_pairs={{0,1},{2,3},{4,5},{6,7},{9,8},{11,10},{13,12},{15,14},{16,17},{18,... | collective-permute-start | bytes 811016 | tf_op jit(solution)/shard_map/ppermute | solution.py:617
  2.0 10.1 %collective-permute-start.4 = (f32[528,128]{1,0:T(8,128)S(1)}, f32[528,128]{1,0:T(8,128)S(1)}, u32[]{:S(2)}, u32[]{:S(2)}) collective-permute-start(f32[528,128]{1,0:T(8,128)S(1)} %get-tuple-element.56), channel_id=1, source_target_pairs={{0,1},{2,3},{4,5},{6,7},{9,8},{11,10},{13,12},{15,14},{16,17},{18,... | collective-permute-start | bytes 811016 | tf_op jit(solution)/shard_map/ppermute | solution.py:617
  3.3 11.7 %collective-permute-start.2 = (f32[528,128]{1,0:T(8,128)S(1)}, f32[528,128]{1,0:T(8,128)S(1)}, u32[]{:S(2)}, u32[]{:S(2)}) collective-permute-start(f32[528,128]{1,0:T(8,128)S(1)} %get-tuple-element.55), channel_id=1, source_target_pairs={{0,1},{2,3},{4,5},{6,7},{9,8},{11,10},{13,12},{15,14},{16,17},{18,... | collective-permute-start | bytes 811016 | tf_op jit(solution)/shard_map/ppermute | solution.py:617
  4.6 13.3 %collective-permute-start = (f32[528,128]{1,0:T(8,128)S(1)}, f32[528,128]{1,0:T(8,128)S(1)}, u32[]{:S(2)}, u32[]{:S(2)}) collective-permute-start(f32[528,128]{1,0:T(8,128)S(1)} %get-tuple-element.51), channel_id=1, source_target_pairs={{0,1},{2,3},{4,5},{6,7},{9,8},{11,10},{13,12},{15,14},{16,17},{18,... | collective-permute-start | bytes 811016 | tf_op jit(solution)/shard_map/ppermute | solution.py:617
  18.4 24.4 %collective-permute-start.16 = (f32[528,512]{1,0:T(8,128)S(1)}, f32[528,512]{1,0:T(8,128)S(1)}, u32[]{:S(2)}, u32[]{:S(2)}) collective-permute-start(f32[528,512]{1,0:T(8,128)S(1)} %get-tuple-element.77), channel_id=1, source_target_pairs={{8,9},{10,11},{12,13},{14,15},{24,25},{26,27},{28,29},{30,31}} | collective-permute-start | bytes 3244040 | tf_op jit(solution)/shard_map/ppermute | solution.py:617
  20.0 7.2 %collective-permute-start.1 = (f32[528,128]{1,0:T(8,128)S(1)}, f32[528,128]{1,0:T(8,128)S(1)}, u32[]{:S(2)}, u32[]{:S(2)}) collective-permute-start(f32[528,128]{1,0:T(8,128)S(1)} %shard_map.70.refs_4_), channel_id=1, source_target_pairs={{1,3},{7,5},{8,10},{14,12},{17,19},{23,21},{24,26},{30,28}} | collective-permute-start | bytes 811016 | tf_op jit(solution)/shard_map/ppermute | solution.py:617
  23.2 6.3 %collective-permute-start.3 = (f32[528,128]{1,0:T(8,128)S(1)}, f32[528,128]{1,0:T(8,128)S(1)}, u32[]{:S(2)}, u32[]{:S(2)}) collective-permute-start(f32[528,128]{1,0:T(8,128)S(1)} %shard_map.71.refs_5_), channel_id=1, source_target_pairs={{1,3},{7,5},{8,10},{14,12},{17,19},{23,21},{24,26},{30,28}} | collective-permute-start | bytes 811016 | tf_op jit(solution)/shard_map/ppermute | solution.py:617
  24.5 7.8 %collective-permute-start.5 = (f32[528,128]{1,0:T(8,128)S(1)}, f32[528,128]{1,0:T(8,128)S(1)}, u32[]{:S(2)}, u32[]{:S(2)}) collective-permute-start(f32[528,128]{1,0:T(8,128)S(1)} %shard_map.72.refs_6_), channel_id=1, source_target_pairs={{1,3},{7,5},{8,10},{14,12},{17,19},{23,21},{24,26},{30,28}} | collective-permute-start | bytes 811016 | tf_op jit(solution)/shard_map/ppermute | solution.py:617
  25.8 9.4 %collective-permute-start.7 = (f32[528,128]{1,0:T(8,128)S(1)}, f32[528,128]{1,0:T(8,128)S(1)}, u32[]{:S(2)}, u32[]{:S(2)}) collective-permute-start(f32[528,128]{1,0:T(8,128)S(1)} %shard_map.73.refs_7_), channel_id=1, source_target_pairs={{1,3},{7,5},{8,10},{14,12},{17,19},{23,21},{24,26},{30,28}} | collective-permute-start | bytes 811016 | tf_op jit(solution)/shard_map/ppermute | solution.py:617
  37.3 1.4 %collective-permute-start.12 = (f32[1056,128]{1,0:T(8,128)S(1)}, f32[1056,128]{1,0:T(8,128)S(1)}, u32[]{:S(2)}, u32[]{:S(2)}) collective-permute-start(f32[1056,128]{1,0:T(8,128)S(1)} %get-tuple-element.70), channel_id=1, source_target_pairs={{3,5},{5,3},{10,12},{12,10},{19,21},{21,19},{26,28},{28,26}} | collective-permute-start | bytes 1622024 | tf_op jit(solution)/shard_map/ppermute | solution.py:617
  38.0 2.9 %collective-permute-start.11 = (f32[1056,128]{1,0:T(8,128)S(1)}, f32[1056,128]{1,0:T(8,128)S(1)}, u32[]{:S(2)}, u32[]{:S(2)}) collective-permute-start(f32[1056,128]{1,0:T(8,128)S(1)} %get-tuple-element.58.refs_0_), channel_id=1, source_target_pairs={{3,5},{5,3},{10,12},{12,10},{19,21},{21,19},{26,28},{28,26}} | collective-permute-start | bytes 1622024 | tf_op jit(solution)/shard_map/ppermute | solution.py:617
  39.3 3.5 %copy-start.1 = (f32[64,512]{1,0:T(8,128)S(1)}, f32[64,512]{1,0:T(8,128)}, u32[]{:S(2)}) copy-start(f32[64,512]{1,0:T(8,128)} %refs_0_.9) | copy-start | bytes 393220
  39.3 4.7 %collective-permute-start.15 = (f32[528,128]{1,0:T(8,128)S(1)}, f32[528,128]{1,0:T(8,128)S(1)}, u32[]{:S(2)}, u32[]{:S(2)}) collective-permute-start(f32[528,128]{1,0:T(8,128)S(1)} %get-tuple-element.72.refs_3_), channel_id=1, source_target_pairs={{3,2},{5,4},{10,11},{12,13},{19,18},{21,20},{26,27},{28,29}} | collective-permute-start | bytes 811016 | tf_op jit(solution)/shard_map/ppermute | solution.py:617
  40.2 3.9 %collective-permute-start.23 = (f32[528,128]{1,0:T(8,128)S(1)}, f32[528,128]{1,0:T(8,128)S(1)}, u32[]{:S(2)}, u32[]{:S(2)}) collective-permute-start(f32[528,128]{1,0:T(8,128)S(1)} %get-tuple-element.71.refs_2_), channel_id=1, source_target_pairs={{3,2},{5,4},{10,11},{12,13},{19,18},{21,20},{26,27},{28,29}} | collective-permute-start | bytes 811016 | tf_op jit(solution)/shard_map/ppermute | solution.py:617
  41.5 2.6 %collective-permute-start.21 = (f32[528,128]{1,0:T(8,128)S(1)}, f32[528,128]{1,0:T(8,128)S(1)}, u32[]{:S(2)}, u32[]{:S(2)}) collective-permute-start(f32[528,128]{1,0:T(8,128)S(1)} %get-tuple-element.68.refs_0_), channel_id=1, source_target_pairs={{3,2},{5,4},{10,11},{12,13},{19,18},{21,20},{26,27},{28,29}} | collective-permute-start | bytes 811016 | tf_op jit(solution)/shard_map/ppermute | solution.py:617
  42.2 1.9 %collective-permute-start.22 = (f32[528,128]{1,0:T(8,128)S(1)}, f32[528,128]{1,0:T(8,128)S(1)}, u32[]{:S(2)}, u32[]{:S(2)}) collective-permute-start(f32[528,128]{1,0:T(8,128)S(1)} %get-tuple-element.69.refs_1_), channel_id=1, source_target_pairs={{3,2},{5,4},{10,11},{12,13},{19,18},{21,20},{26,27},{28,29}} | collective-permute-start | bytes 811016 | tf_op jit(solution)/shard_map/ppermute | solution.py:617
  42.9 1.6 %collective-permute-start.20 = (f32[64,512]{1,0:T(8,128)S(1)}, f32[64,512]{1,0:T(8,128)S(1)}, u32[]{:S(2)}, u32[]{:S(2)}) collective-permute-start(f32[64,512]{1,0:T(8,128)S(1)} %copy-done.1), channel_id=1, source_target_pairs={{0,2},{1,3},{6,4},{7,5}} | collective-permute-start | bytes 393224 | tf_op jit(solution)/shard_map/ppermute | solution.py:617
  44.4 0.7 collective-permute-start.24
  45.5 0.7 collective-permute-start.25
  46.6 2.4 %copy-start.2 = (f32[4,512]{1,0:T(4,128)S(1)}, f32[4,512]{1,0:T(4,128)}, u32[]{:S(2)}) copy-start(f32[4,512]{1,0:T(4,128)} %refs_0_.8) | copy-start | bytes 24580
  46.6 0.7 collective-permute-start.26
  47.7 51.9 %collective-permute-start.27 = (f32[64,512]{1,0:T(8,128)S(1)}, f32[64,512]{1,0:T(8,128)S(1)}, u32[]{:S(2)}, u32[]{:S(2)}) collective-permute-start(f32[64,512]{1,0:T(8,128)S(1)} %get-tuple-element.99), channel_id=1, source_target_pairs={{2,0},{3,1},{4,6},{5,7},{10,8},{11,9},{12,14},{13,15},{18,16},{19,... | collective-permute-start | bytes 393224 | tf_op jit(solution)/shard_map/ppermute | solution.py:617
  49.3 0.7 collective-permute-start.8
  50.2 1.3 %collective-permute-start.10 = (f32[8,512]{1,0:T(8,128)S(1)}, f32[8,512]{1,0:T(8,128)S(1)}, u32[]{:S(2)}, u32[]{:S(2)}) collective-permute-start(f32[8,512]{1,0:T(8,128)S(1)} %shard_map.77), channel_id=1, source_target_pairs={{5,10}} | collective-permute-start | bytes 49160 | tf_op jit(solution)/shard_map/ppermute | solution.py:617
  50.9 0.7 collective-permute-start.9
  52.1 0.7 collective-permute-start.13
  53.1 45.6 %copy-start = (bf16[2,512,512]{2,1,0:T(8,128)(2,1)S(1)}, bf16[2,512,512]{2,1,0:T(8,128)(2,1)}, u32[]{:S(2)}) copy-start(bf16[2,512,512]{2,1,0:T(8,128)(2,1)} %refs_7_.1) | copy-start | bytes 3145732
  53.1 0.8 collective-permute-start.14
  54.2 2.6 %collective-permute-start.19 = (f32[8,512]{1,0:T(8,128)S(1)}, f32[8,512]{1,0:T(8,128)S(1)}, u32[]{:S(2)}, u32[]{:S(2)}) collective-permute-start(f32[8,512]{1,0:T(8,128)S(1)} %get-tuple-element.87.refs_0_), channel_id=1, source_target_pairs={{3,2},{5,4},{10,11},{12,13},{19,18},{21,20},{26,27},{28,29}} | collective-permute-start | bytes 49160 | tf_op jit(solution)/shard_map/ppermute | solution.py:617
  54.8 2.0 %collective-permute-start.18 = (f32[8,512]{1,0:T(8,128)S(1)}, f32[8,512]{1,0:T(8,128)S(1)}, u32[]{:S(2)}, u32[]{:S(2)}) collective-permute-start(f32[8,512]{1,0:T(8,128)S(1)} %get-tuple-element.88), channel_id=1, source_target_pairs={{3,0},{5,6},{10,9},{12,15},{19,16},{21,22},{26,25},{28,31}} | collective-permute-start | bytes 49160 | tf_op jit(solution)/shard_map/ppermute | solution.py:617
  55.5 43.2 %collective-permute-start.17 = (f32[8,512]{1,0:T(8,128)S(1)}, f32[8,512]{1,0:T(8,128)S(1)}, u32[]{:S(2)}, u32[]{:S(2)}) collective-permute-start(f32[8,512]{1,0:T(8,128)S(1)} %get-tuple-element.88), channel_id=1, source_target_pairs={{3,1},{5,7},{10,8},{12,14},{19,17},{21,23},{26,24},{28,30}} | collective-permute-start | bytes 49160 | tf_op jit(solution)/shard_map/ppermute | solution.py:617
where the time goes:
time: 101 us; the launch traced here: 100 us
  waiting for transfers between devices  57.8 us (57%)
  starting transfers between devices  28.2 us (28%)
  Pallas kernels  13.2 us (13%)
  between operations  1.18 us (1%)
    ppermute x28, waiting for transfers between devices, send(): return lax.ppermute(x, AXES, pairs)  57.8 us
    ppermute x28, starting transfers between devices, send(): return lax.ppermute(x, AXES, pairs)  28.2 us
    pallas_call x25, Pallas kernels, call(): pl.pallas_call(body, out_shape=outs, in_specs=in_specs, out_specs=jax.tre...  13.2 us
  transfers between devices with their start and end apart: 28, of which 8 were waited for; matrix products, arithmetic and copies ran while one was open for 0% of the time, Pallas kernels for 11%

commit v1 on v0

--- a/solution.py
+++ b/solution.py
@@ -446,6 +446,19 @@
     return res if split else res[0]
 
 
+def pick(where, one, two):
+    def kernel(flag, a, b, out):
+        @pl.when(flag)
+        def _():
+            out[...] = a[...]
+
+        @pl.when(jnp.logical_not(flag))
+        def _():
+            out[...] = b[...]
+
+    return call(kernel, shape(*one.shape), [one, two], where)
+
+
 def advance_mean(z, mean, block):
     low = padded(z.series)
 
@@ -658,11 +671,17 @@
         whole, own_map, late = local_map(z, receives, transition, obs_gain, observed, False)
         outs = [one_chunk(c) for c in first]
         back = send(tied(whole, outs), tree.pairs(lambda odd: [(i, i + 1) for i in range(0, size, 2)] if odd else []))
-        bits = [1 << i for i in range(depth - 3, -1, -1)]
-        start = [init_factor]
+        order, bits = [0], [1 << i for i in range(depth - 3, -1, -1)]
         for bit in bits:
-            held = start[0] if len(start) == 1 else jnp.concatenate(start)
-            start = [held, send(tied(held, outs), tree.far(bit, 0))]
+            order += [o ^ bit for o in order]
+        rows_in = tied(init_factor, outs)
+        start = []
+        for away in [2 * o for o in order] + [2 * o ^ 1 for o in order]:
+            if away == 0:
+                start.append(init_factor)
+            else:
+                pairs = [(r ^ away, r) for r in tree.child_roots(0, depth, 0)]
+                start.append(send(rows_in, pairs))
         lefts = {}
         for level in range(2, depth):
 
@@ -685,6 +704,7 @@
         nexts = [(b, size + r) for r in tree.child_roots(1, depth, 0)]
         second = send(onward, nexts[1:]) + send(onward, nexts[:1])
         roots = tree.pairs(lambda odd: [(r, r ^ 1) for r in tree.child_roots(odd, depth, 0)])
+        roots = [p for p in roots if p[0] >= size]
         got = [send(c, roots) for c in final]
         left = assemble(z, lambda seg, tm: (seg >= 0, seg % 2 == 1), first, [back])
         halfway = assemble(z, lambda seg, tm: (seg >= 0, seg < 0), crossed)
@@ -705,33 +725,46 @@
             gone = advance_mean(z, entries[-1], at_root)
             entries.append(send(gone, pairs))
 
-        moved = advance(z, lambda seg, tm: seg == 0, start, block)
+        same, aside = advance(z, lambda seg, tm: seg == 0, start, at_root, split=True)
+        first_roots = tree.child_roots(0, depth, 0)
+        moved = pick(
+            lambda seg, tm: tm == tree.root_of(0, depth - 1, tm // half),
+            same,
+            send(aside, [(r, r ^ 1) for r in first_roots]),
+        )
         for turn in range(1, segs):
             pairs = [((turn - 1) * size + i, turn * size + i) for i in range(size) if tree.holds(i)]
-            arrived = send(moved, pairs)
+            if turn == 1:
+                arrived = send(same, [(r, size + r) for r in first_roots])
+                arrived = arrived + send(aside, [(r, size + (r ^ 1)) for r in first_roots])
+            else:
+                arrived = send(moved, pairs)
 
             def where(seg, tm, turn=turn):
                 return seg >= turn
 
             moved = advance(z, where, [arrived], block, moved, turn == segs - 1)
 
-        def down(arrivals):
+        def down(arrivals, first_seg, last_seg):
+            def only(pairs):
+                return [p for p in pairs if first_seg <= p[0] // size <= last_seg]
+
             candidates, cross = arrivals, halfway
             for level in range(depth - 1, 1, -1):
 
                 def where(seg, tm, level=level):
                     if level == depth - 1:
-                        index = seg
+                        index = seg - first_seg
                     else:
                         index = (tm == top_and_other(seg, tm, level + 1)[1]).astype(jnp.int32)
                     return index, tm >= half, (tm >> level) % 2 == 0
 
                 mine_in, other_in = descend(z, where, candidates, lefts[level], cross)
-                candidates, cross = [mine_in, send(other_in, others(level, 0))], None
+                candidates, cross = [mine_in, send(other_in, only(others(level, 0)))], None
             near = tree.pairs(lambda odd: [(tree.root(odd, 2, g), tree.root(odd, 2, g) ^ 1) for g in range(size >> 2)])
-            return [*candidates, send(other_in, others(2, 1)), send(mine_in, near)]
-
-        candidates = down(entries)
+            return [*candidates, send(other_in, only(others(2, 1))), send(mine_in, only(near))]
+
+        candidates = down(entries[:-1], 0, segs - 2) + down(entries[-1:], segs - 1, segs - 1)
 
         kept, given = moved
         for bit in reversed(bits):
@@ -751,6 +784,7 @@
         def where(seg, tm):
             top, other = top_and_other(seg, tm, 2)
             index = jnp.where(tm == other, 1, jnp.where(tm == other ^ 1, 2, jnp.where(tm == top, 0, 3)))
+            index = index + jnp.where(seg == segs - 1, 4, 0)
             return index, tm % 2 == 1, (seg + tm) % 2 == 1
 
         return last_steps(z, where, candidates, left, transition, (early, late)), ends

time: 101 us -> 97.8 us (0.968)
  waiting for transfers between devices: 57.8 us -> 46.7 us
  starting transfers between devices: 28.2 us -> 35.4 us
    ppermute x28 -> x35, waiting for transfers between devices: 57.8 us -> 46.7 us  [send(): return lax.ppermute(x, AXES, pairs)]
    ppermute x28 -> x35, starting transfers between devices: 28.2 us -> 35.4 us  [send(): return lax.ppermute(x, AXES, pairs)]
    pallas_call x25 -> x27, Pallas kernels: 13.2 us -> 13.7 us  [call(): pl.pallas_call(body, out_shape=outs, in_specs=in_specs, out_specs=jax.tre...]
  transfers between devices with their start and end apart: 28 -> 35, of which waited for: 8 -> 5; matrix products, arithmetic and copies ran while one was open for 0% -> 0% of each run, Pallas kernels for 11% -> 10%
where the time goes in v1:
time: 97.8 us; the launch traced here: 97.1 us
  waiting for transfers between devices  46.7 us (48%)
  starting transfers between devices  35.4 us (36%)
  Pallas kernels  13.7 us (14%)
  between operations  1.33 us (1%)
    ppermute x35, waiting for transfers between devices, send(): return lax.ppermute(x, AXES, pairs)  46.7 us
    ppermute x35, starting transfers between devices, send(): return lax.ppermute(x, AXES, pairs)  35.4 us
    pallas_call x27, Pallas kernels, call(): pl.pallas_call(body, out_shape=outs, in_specs=in_specs, out_specs=jax.tre...  13.7 us
  transfers between devices with their start and end apart: 35, of which 5 were waited for; matrix products, arithmetic and copies ran while one was open for 0% of the time, Pallas kernels for 10%

profile of v1, /device:TPU:5, one launch (start us, length us, event | category | flops | bytes accessed | tf_op | source)
XLA Modules:
  0.0 97.1 jit_solution(6337041066260203557)
XLA Ops:
  0.7 1.3 %collective-permute-start = (f32[528,128]{1,0:T(8,128)S(1)}, f32[528,128]{1,0:T(8,128)S(1)}, u32[]{:S(2)}, u32[]{:S(2)}) collective-permute-start(f32[528,128]{1,0:T(8,128)S(1)} %get-tuple-element.55), channel_id=1, source_target_pairs={{0,1},{2,3},{4,5},{6,7},{9,8},{11,10},{13,12},{15,14},{16,17},{18,... | collective-permute-start | bytes 811016 | tf_op jit(solution)/shard_map/ppermute | solution.py:630
  2.0 1.3 %collective-permute-start.2 = (f32[528,128]{1,0:T(8,128)S(1)}, f32[528,128]{1,0:T(8,128)S(1)}, u32[]{:S(2)}, u32[]{:S(2)}) collective-permute-start(f32[528,128]{1,0:T(8,128)S(1)} %get-tuple-element.59), channel_id=1, source_target_pairs={{0,1},{2,3},{4,5},{6,7},{9,8},{11,10},{13,12},{15,14},{16,17},{18,... | collective-permute-start | bytes 811016 | tf_op jit(solution)/shard_map/ppermute | solution.py:630
  3.3 1.3 %collective-permute-start.4 = (f32[528,128]{1,0:T(8,128)S(1)}, f32[528,128]{1,0:T(8,128)S(1)}, u32[]{:S(2)}, u32[]{:S(2)}) collective-permute-start(f32[528,128]{1,0:T(8,128)S(1)} %get-tuple-element.60), channel_id=1, source_target_pairs={{0,1},{2,3},{4,5},{6,7},{9,8},{11,10},{13,12},{15,14},{16,17},{18,... | collective-permute-start | bytes 811016 | tf_op jit(solution)/shard_map/ppermute | solution.py:630
  4.6 1.3 %collective-permute-start.6 = (f32[528,128]{1,0:T(8,128)S(1)}, f32[528,128]{1,0:T(8,128)S(1)}, u32[]{:S(2)}, u32[]{:S(2)}) collective-permute-start(f32[528,128]{1,0:T(8,128)S(1)} %get-tuple-element.61), channel_id=1, source_target_pairs={{0,1},{2,3},{4,5},{6,7},{9,8},{11,10},{13,12},{15,14},{16,17},{18,... | collective-permute-start | bytes 811016 | tf_op jit(solution)/shard_map/ppermute | solution.py:630
  5.9 2.4 %shard_map.69 = (f32[528,512]{1,0:T(8,128)S(1)}, bf16[528,512]{1,0:T(8,128)(2,1)S(1)}, bf16[528,512]{1,0:T(8,128)(2,1)S(1)}, f32[4,512]{1,0:T(4,128)S(1)}, f32[2,4,512]{2,1,0:T(4,128)S(1)}) custom-call(bf16[2,512,512]{2,1,0:T(8,128)(2,1)} %refs_11_.1, bf16[2,512,512]{2,1,0:T(8,128)(2,1)} %refs_1_.3, bf16[2,4,512]{2,1,0:T(4,128)(2,1)} %refs_2_.3), custom_call_target="tpu_custom_call" | custom-call | tf_op jit(solution)/shard_map/pallas_call | solution.py:101
  8.3 0.9 collective-permute-done.refs_0_
  9.8 3.2 %collective-permute-start.1 = (f32[528,128]{1,0:T(8,128)S(1)}, f32[528,128]{1,0:T(8,128)S(1)}, u32[]{:S(2)}, u32[]{:S(2)}) collective-permute-start(f32[528,128]{1,0:T(8,128)S(1)} %shard_map.70.refs_4_), channel_id=1, source_target_pairs={{1,3},{7,5},{8,10},{14,12},{17,19},{23,21},{24,26},{30,28}} | collective-permute-start | bytes 811016 | tf_op jit(solution)/shard_map/ppermute | solution.py:630
  13.6 2.3 %collective-permute-start.3 = (f32[528,128]{1,0:T(8,128)S(1)}, f32[528,128]{1,0:T(8,128)S(1)}, u32[]{:S(2)}, u32[]{:S(2)}) collective-permute-start(f32[528,128]{1,0:T(8,128)S(1)} %shard_map.71.refs_5_), channel_id=1, source_target_pairs={{1,3},{7,5},{8,10},{14,12},{17,19},{23,21},{24,26},{30,28}} | collective-permute-start | bytes 811016 | tf_op jit(solution)/shard_map/ppermute | solution.py:630
  16.5 2.3 %collective-permute-start.5 = (f32[528,128]{1,0:T(8,128)S(1)}, f32[528,128]{1,0:T(8,128)S(1)}, u32[]{:S(2)}, u32[]{:S(2)}) collective-permute-start(f32[528,128]{1,0:T(8,128)S(1)} %shard_map.72.refs_6_), channel_id=1, source_target_pairs={{1,3},{7,5},{8,10},{14,12},{17,19},{23,21},{24,26},{30,28}} | collective-permute-start | bytes 811016 | tf_op jit(solution)/shard_map/ppermute | solution.py:630
  19.4 2.3 %collective-permute-start.7 = (f32[528,128]{1,0:T(8,128)S(1)}, f32[528,128]{1,0:T(8,128)S(1)}, u32[]{:S(2)}, u32[]{:S(2)}) collective-permute-start(f32[528,128]{1,0:T(8,128)S(1)} %shard_map.73.refs_7_), channel_id=1, source_target_pairs={{1,3},{7,5},{8,10},{14,12},{17,19},{23,21},{24,26},{30,28}} | collective-permute-start | bytes 811016 | tf_op jit(solution)/shard_map/ppermute | solution.py:630
  22.1 2.9 %collective-permute-done.7.refs_3_ = f32[528,128]{1,0:T(8,128)S(1)} collective-permute-done((f32[528,128]{1,0:T(8,128)S(1)}, f32[528,128]{1,0:T(8,128)S(1)}, u32[]{:S(2)}, u32[]{:S(2)}) %collective-permute-start.7) | collective-permute-done | bytes 270368 | tf_op jit(solution)/shard_map/ppermute | solution.py:630
  25.0 1.2 %shard_map.74 = (f32[1056,128]{1,0:T(8,128)S(1)}, bf16[528,512]{1,0:T(8,128)(2,1)S(1)}, bf16[528,512]{1,0:T(8,128)(2,1)S(1)}, f32[4,512]{1,0:T(4,128)S(1)}, bf16...) custom-call(f32[528,128]{1,0:T(8,128)S(1)} %collective-permute-done.1.refs_0_, ...), custom_call_target="tpu_custom_call" | custom-call | tf_op jit(solution)/shard_map/pallas_call | solution.py:101
  26.3 0.8 shard_map.75
  27.1 0.7 collective-permute-start.12
  27.8 1.4 %collective-permute-start.15 = (f32[528,512]{1,0:T(8,128)S(1)}, f32[528,512]{1,0:T(8,128)S(1)}, u32[]{:S(2)}, u32[]{:S(2)}) collective-permute-start(f32[528,512]{1,0:T(8,128)S(1)} %get-tuple-element.81), channel_id=1, source_target_pairs={{8,9},{10,11},{12,13},{14,15},{24,25},{26,27},{28,29},{30,31}} | collective-permute-start | bytes 3244040 | tf_op jit(solution)/shard_map/ppermute | solution.py:630
  29.1 0.7 collective-permute-start.11
  29.9 0.7 collective-permute-start.25
  33.5 0.7 collective-permute-start.26
  34.2 0.7 collective-permute-start.31
  34.9 0.7 collective-permute-start.27
  35.6 0.7 collective-permute-start.14
  36.3 0.7 collective-permute-start.30
  37.0 0.7 collective-permute-start.28
  37.7 0.7 collective-permute-start.29
  38.7 2.5 %collective-permute-done.15.refs_4_ = f32[528,512]{1,0:T(8,128)S(1)} collective-permute-done((f32[528,512]{1,0:T(8,128)S(1)}, f32[528,512]{1,0:T(8,128)S(1)}, u32[]{:S(2)}, u32[]{:S(2)}) %collective-permute-start.15) | collective-permute-done | bytes 1081376 | tf_op jit(solution)/shard_map/ppermute | solution.py:630
  42.3 0.7 collective-permute-start.32
  43.4 0.7 collective-permute-start.33
  44.5 1.3 %collective-permute-start.34 = (f32[64,512]{1,0:T(8,128)S(1)}, f32[64,512]{1,0:T(8,128)S(1)}, u32[]{:S(2)}, u32[]{:S(2)}) collective-permute-start(f32[64,512]{1,0:T(8,128)S(1)} %get-tuple-element.107), channel_id=1, source_target_pairs={{2,0},{3,1},{4,6},{5,7},{10,8},{11,9},{12,14},{13,15},{18,16},{19,... | collective-permute-start | bytes 393224 | tf_op jit(solution)/shard_map/ppermute | solution.py:630
  51.2 0.8 collective-permute-start.17
  54.3 1.3 %collective-permute-start.20 = (f32[8,512]{1,0:T(8,128)S(1)}, f32[8,512]{1,0:T(8,128)S(1)}, u32[]{:S(2)}, u32[]{:S(2)}) collective-permute-start(f32[8,512]{1,0:T(8,128)S(1)} %get-tuple-element.94), channel_id=1, source_target_pairs={{26,24},{28,30}} | collective-permute-start | bytes 49160 | tf_op jit(solution)/shard_map/ppermute | solution.py:630
  55.6 39.9 %collective-permute-done.20.refs_5_ = f32[8,512]{1,0:T(8,128)S(1)} collective-permute-done((f32[8,512]{1,0:T(8,128)S(1)}, f32[8,512]{1,0:T(8,128)S(1)}, u32[]{:S(2)}, u32[]{:S(2)}) %collective-permute-start.20) | collective-permute-done | bytes 16416 | tf_op jit(solution)/shard_map/ppermute | solution.py:630
  95.5 1.0 shard_map.87
  (73 shorter events, 16.3 us)
Async XLA Ops:
  0.7 8.5 %collective-permute-start = (f32[528,128]{1,0:T(8,128)S(1)}, f32[528,128]{1,0:T(8,128)S(1)}, u32[]{:S(2)}, u32[]{:S(2)}) collective-permute-start(f32[528,128]{1,0:T(8,128)S(1)} %get-tuple-element.55), channel_id=1, source_target_pairs={{0,1},{2,3},{4,5},{6,7},{9,8},{11,10},{13,12},{15,14},{16,17},{18,... | collective-permute-start | bytes 811016 | tf_op jit(solution)/shard_map/ppermute | solution.py:630
  2.0 11.0 %collective-permute-start.2 = (f32[528,128]{1,0:T(8,128)S(1)}, f32[528,128]{1,0:T(8,128)S(1)}, u32[]{:S(2)}, u32[]{:S(2)}) collective-permute-start(f32[528,128]{1,0:T(8,128)S(1)} %get-tuple-element.59), channel_id=1, source_target_pairs={{0,1},{2,3},{4,5},{6,7},{9,8},{11,10},{13,12},{15,14},{16,17},{18,... | collective-permute-start | bytes 811016 | tf_op jit(solution)/shard_map/ppermute | solution.py:630
  3.3 12.6 %collective-permute-start.4 = (f32[528,128]{1,0:T(8,128)S(1)}, f32[528,128]{1,0:T(8,128)S(1)}, u32[]{:S(2)}, u32[]{:S(2)}) collective-permute-start(f32[528,128]{1,0:T(8,128)S(1)} %get-tuple-element.60), channel_id=1, source_target_pairs={{0,1},{2,3},{4,5},{6,7},{9,8},{11,10},{13,12},{15,14},{16,17},{18,... | collective-permute-start | bytes 811016 | tf_op jit(solution)/shard_map/ppermute | solution.py:630
  4.6 14.2 %collective-permute-start.6 = (f32[528,128]{1,0:T(8,128)S(1)}, f32[528,128]{1,0:T(8,128)S(1)}, u32[]{:S(2)}, u32[]{:S(2)}) collective-permute-start(f32[528,128]{1,0:T(8,128)S(1)} %get-tuple-element.61), channel_id=1, source_target_pairs={{0,1},{2,3},{4,5},{6,7},{9,8},{11,10},{13,12},{15,14},{16,17},{18,... | collective-permute-start | bytes 811016 | tf_op jit(solution)/shard_map/ppermute | solution.py:630
  9.8 11.9 %collective-permute-start.1 = (f32[528,128]{1,0:T(8,128)S(1)}, f32[528,128]{1,0:T(8,128)S(1)}, u32[]{:S(2)}, u32[]{:S(2)}) collective-permute-start(f32[528,128]{1,0:T(8,128)S(1)} %shard_map.70.refs_4_), channel_id=1, source_target_pairs={{1,3},{7,5},{8,10},{14,12},{17,19},{23,21},{24,26},{30,28}} | collective-permute-start | bytes 811016 | tf_op jit(solution)/shard_map/ppermute | solution.py:630
  13.6 8.1 %collective-permute-start.3 = (f32[528,128]{1,0:T(8,128)S(1)}, f32[528,128]{1,0:T(8,128)S(1)}, u32[]{:S(2)}, u32[]{:S(2)}) collective-permute-start(f32[528,128]{1,0:T(8,128)S(1)} %shard_map.71.refs_5_), channel_id=1, source_target_pairs={{1,3},{7,5},{8,10},{14,12},{17,19},{23,21},{24,26},{30,28}} | collective-permute-start | bytes 811016 | tf_op jit(solution)/shard_map/ppermute | solution.py:630
  16.5 5.6 %collective-permute-start.5 = (f32[528,128]{1,0:T(8,128)S(1)}, f32[528,128]{1,0:T(8,128)S(1)}, u32[]{:S(2)}, u32[]{:S(2)}) collective-permute-start(f32[528,128]{1,0:T(8,128)S(1)} %shard_map.72.refs_6_), channel_id=1, source_target_pairs={{1,3},{7,5},{8,10},{14,12},{17,19},{23,21},{24,26},{30,28}} | collective-permute-start | bytes 811016 | tf_op jit(solution)/shard_map/ppermute | solution.py:630
  19.4 5.6 %collective-permute-start.7 = (f32[528,128]{1,0:T(8,128)S(1)}, f32[528,128]{1,0:T(8,128)S(1)}, u32[]{:S(2)}, u32[]{:S(2)}) collective-permute-start(f32[528,128]{1,0:T(8,128)S(1)} %shard_map.73.refs_7_), channel_id=1, source_target_pairs={{1,3},{7,5},{8,10},{14,12},{17,19},{23,21},{24,26},{30,28}} | collective-permute-start | bytes 811016 | tf_op jit(solution)/shard_map/ppermute | solution.py:630
  27.1 4.1 %collective-permute-start.12 = (f32[1056,128]{1,0:T(8,128)S(1)}, f32[1056,128]{1,0:T(8,128)S(1)}, u32[]{:S(2)}, u32[]{:S(2)}) collective-permute-start(f32[1056,128]{1,0:T(8,128)S(1)} %get-tuple-element.74), channel_id=1, source_target_pairs={{3,5},{5,3},{10,12},{12,10},{19,21},{21,19},{26,28},{28,26}} | collective-permute-start | bytes 1622024 | tf_op jit(solution)/shard_map/ppermute | solution.py:630
  27.8 13.4 %collective-permute-start.15 = (f32[528,512]{1,0:T(8,128)S(1)}, f32[528,512]{1,0:T(8,128)S(1)}, u32[]{:S(2)}, u32[]{:S(2)}) collective-permute-start(f32[528,512]{1,0:T(8,128)S(1)} %get-tuple-element.81), channel_id=1, source_target_pairs={{8,9},{10,11},{12,13},{14,15},{24,25},{26,27},{28,29},{30,31}} | collective-permute-start | bytes 3244040 | tf_op jit(solution)/shard_map/ppermute | solution.py:630
  29.1 3.4 %collective-permute-start.11 = (f32[1056,128]{1,0:T(8,128)S(1)}, f32[1056,128]{1,0:T(8,128)S(1)}, u32[]{:S(2)}, u32[]{:S(2)}) collective-permute-start(f32[1056,128]{1,0:T(8,128)S(1)} %get-tuple-element.62.refs_0_), channel_id=1, source_target_pairs={{3,5},{5,3},{10,12},{12,10},{19,21},{21,19},{26,28},{28,26}} | collective-permute-start | bytes 1622024 | tf_op jit(solution)/shard_map/ppermute | solution.py:630
  29.9 3.6 %collective-permute-start.25 = (f32[64,512]{1,0:T(8,128)S(1)}, f32[64,512]{1,0:T(8,128)S(1)}, u32[]{:S(2)}, u32[]{:S(2)}) collective-permute-start(f32[64,512]{1,0:T(8,128)S(1)} %copy-done.1), channel_id=1, source_target_pairs={{0,3},{6,5}} | collective-permute-start | bytes 393224 | tf_op jit(solution)/shard_map/ppermute | solution.py:630
  30.5 2.9 %collective-permute-start.24 = (f32[64,512]{1,0:T(8,128)S(1)}, f32[64,512]{1,0:T(8,128)S(1)}, u32[]{:S(2)}, u32[]{:S(2)}) collective-permute-start(f32[64,512]{1,0:T(8,128)S(1)} %copy-done.1), channel_id=1, source_target_pairs={{2,3},{4,5}} | collective-permute-start | bytes 393224 | tf_op jit(solution)/shard_map/ppermute | solution.py:630
  31.2 2.3 %collective-permute-start.23 = (f32[64,512]{1,0:T(8,128)S(1)}, f32[64,512]{1,0:T(8,128)S(1)}, u32[]{:S(2)}, u32[]{:S(2)}) collective-permute-start(f32[64,512]{1,0:T(8,128)S(1)} %copy-done.1), channel_id=1, source_target_pairs={{1,3},{7,5}} | collective-permute-start | bytes 393224 | tf_op jit(solution)/shard_map/ppermute | solution.py:630
  33.5 2.7 %collective-permute-start.26 = (f32[128,512]{1,0:T(8,128)S(1)}, f32[128,512]{1,0:T(8,128)S(1)}, u32[]{:S(2)}, u32[]{:S(2)}) collective-permute-start(f32[128,512]{1,0:T(8,128)S(1)} %get-tuple-element.101.refs_0_), channel_id=1, source_target_pairs={{3,11},{5,13}} | collective-permute-start | bytes 786440 | tf_op jit(solution)/shard_map/ppermute | solution.py:630
  34.2 2.8 %collective-permute-start.31 = (f32[128,512]{1,0:T(8,128)S(1)}, f32[128,512]{1,0:T(8,128)S(1)}, u32[]{:S(2)}, u32[]{:S(2)}) collective-permute-start(f32[128,512]{1,0:T(8,128)S(1)} %get-tuple-element.102), channel_id=1, source_target_pairs={{3,2},{5,4}} | collective-permute-start | bytes 786440 | tf_op jit(solution)/shard_map/ppermute | solution.py:630
  34.9 2.8 %collective-permute-start.27 = (f32[128,512]{1,0:T(8,128)S(1)}, f32[128,512]{1,0:T(8,128)S(1)}, u32[]{:S(2)}, u32[]{:S(2)}) collective-permute-start(f32[128,512]{1,0:T(8,128)S(1)} %get-tuple-element.102), channel_id=1, source_target_pairs={{3,10},{5,12}} | collective-permute-start | bytes 786440 | tf_op jit(solution)/shard_map/ppermute | solution.py:630
  35.6 5.8 %collective-permute-start.14 = (f32[528,128]{1,0:T(8,128)S(1)}, f32[528,128]{1,0:T(8,128)S(1)}, u32[]{:S(2)}, u32[]{:S(2)}) collective-permute-start(f32[528,128]{1,0:T(8,128)S(1)} %get-tuple-element.76.refs_3_), channel_id=1, source_target_pairs={{10,11},{12,13},{19,18},{21,20},{26,27},{28,29}} | collective-permute-start | bytes 811016 | tf_op jit(solution)/shard_map/ppermute | solution.py:630
  36.3 5.1 %collective-permute-start.30 = (f32[528,128]{1,0:T(8,128)S(1)}, f32[528,128]{1,0:T(8,128)S(1)}, u32[]{:S(2)}, u32[]{:S(2)}) collective-permute-start(f32[528,128]{1,0:T(8,128)S(1)} %get-tuple-element.75.refs_2_), channel_id=1, source_target_pairs={{10,11},{12,13},{19,18},{21,20},{26,27},{28,29}} | collective-permute-start | bytes 811016 | tf_op jit(solution)/shard_map/ppermute | solution.py:630
  37.0 4.4 %collective-permute-start.28 = (f32[528,128]{1,0:T(8,128)S(1)}, f32[528,128]{1,0:T(8,128)S(1)}, u32[]{:S(2)}, u32[]{:S(2)}) collective-permute-start(f32[528,128]{1,0:T(8,128)S(1)} %get-tuple-element.72.refs_0_), channel_id=1, source_target_pairs={{10,11},{12,13},{19,18},{21,20},{26,27},{28,29}} | collective-permute-start | bytes 811016 | tf_op jit(solution)/shard_map/ppermute | solution.py:630
  37.7 3.8 %collective-permute-start.29 = (f32[528,128]{1,0:T(8,128)S(1)}, f32[528,128]{1,0:T(8,128)S(1)}, u32[]{:S(2)}, u32[]{:S(2)}) collective-permute-start(f32[528,128]{1,0:T(8,128)S(1)} %get-tuple-element.73.refs_1_), channel_id=1, source_target_pairs={{10,11},{12,13},{19,18},{21,20},{26,27},{28,29}} | collective-permute-start | bytes 811016 | tf_op jit(solution)/shard_map/ppermute | solution.py:630
  42.3 0.7 collective-permute-start.32
  43.4 0.7 collective-permute-start.33
  44.5 52.0 %collective-permute-start.34 = (f32[64,512]{1,0:T(8,128)S(1)}, f32[64,512]{1,0:T(8,128)S(1)}, u32[]{:S(2)}, u32[]{:S(2)}) collective-permute-start(f32[64,512]{1,0:T(8,128)S(1)} %get-tuple-element.107), channel_id=1, source_target_pairs={{2,0},{3,1},{4,6},{5,7},{10,8},{11,9},{12,14},{13,15},{18,16},{19,... | collective-permute-start | bytes 393224 | tf_op jit(solution)/shard_map/ppermute | solution.py:630
  47.0 1.3 %collective-permute-start.10 = (f32[8,512]{1,0:T(8,128)S(1)}, f32[8,512]{1,0:T(8,128)S(1)}, u32[]{:S(2)}, u32[]{:S(2)}) collective-permute-start(f32[8,512]{1,0:T(8,128)S(1)} %shard_map.77), channel_id=1, source_target_pairs={{5,10}} | collective-permute-start | bytes 49160 | tf_op jit(solution)/shard_map/ppermute | solution.py:630
  49.5 3.1 %collective-permute-start.19 = (f32[8,512]{1,0:T(8,128)S(1)}, f32[8,512]{1,0:T(8,128)S(1)}, u32[]{:S(2)}, u32[]{:S(2)}) collective-permute-start(f32[8,512]{1,0:T(8,128)S(1)} %shard_map.85), channel_id=1, source_target_pairs={{19,26},{21,28}} | collective-permute-start | bytes 49160 | tf_op jit(solution)/shard_map/ppermute | solution.py:630
  50.5 3.1 %collective-permute-start.18 = (f32[8,512]{1,0:T(8,128)S(1)}, f32[8,512]{1,0:T(8,128)S(1)}, u32[]{:S(2)}, u32[]{:S(2)}) collective-permute-start(f32[8,512]{1,0:T(8,128)S(1)} %get-tuple-element.91.refs_0_), channel_id=1, source_target_pairs={{3,2},{5,4},{10,11},{12,13},{19,18},{21,20}} | collective-permute-start | bytes 49160 | tf_op jit(solution)/shard_map/ppermute | solution.py:630
  51.2 3.1 %collective-permute-start.17 = (f32[8,512]{1,0:T(8,128)S(1)}, f32[8,512]{1,0:T(8,128)S(1)}, u32[]{:S(2)}, u32[]{:S(2)}) collective-permute-start(f32[8,512]{1,0:T(8,128)S(1)} %get-tuple-element.92), channel_id=1, source_target_pairs={{3,0},{5,6},{10,9},{12,15},{19,16},{21,22}} | collective-permute-start | bytes 49160 | tf_op jit(solution)/shard_map/ppermute | solution.py:630
  52.0 3.6 %collective-permute-start.16 = (f32[8,512]{1,0:T(8,128)S(1)}, f32[8,512]{1,0:T(8,128)S(1)}, u32[]{:S(2)}, u32[]{:S(2)}) collective-permute-start(f32[8,512]{1,0:T(8,128)S(1)} %get-tuple-element.92), channel_id=1, source_target_pairs={{3,1},{5,7},{10,8},{12,14},{19,17},{21,23}} | collective-permute-start | bytes 49160 | tf_op jit(solution)/shard_map/ppermute | solution.py:630
  52.9 2.7 %collective-permute-start.22 = (f32[8,512]{1,0:T(8,128)S(1)}, f32[8,512]{1,0:T(8,128)S(1)}, u32[]{:S(2)}, u32[]{:S(2)}) collective-permute-start(f32[8,512]{1,0:T(8,128)S(1)} %get-tuple-element.93.refs_4_), channel_id=1, source_target_pairs={{26,27},{28,29}} | collective-permute-start | bytes 49160 | tf_op jit(solution)/shard_map/ppermute | solution.py:630
  53.6 2.0 %collective-permute-start.21 = (f32[8,512]{1,0:T(8,128)S(1)}, f32[8,512]{1,0:T(8,128)S(1)}, u32[]{:S(2)}, u32[]{:S(2)}) collective-permute-start(f32[8,512]{1,0:T(8,128)S(1)} %get-tuple-element.94), channel_id=1, source_target_pairs={{26,25},{28,31}} | collective-permute-start | bytes 49160 | tf_op jit(solution)/shard_map/ppermute | solution.py:630
  54.3 41.2 %collective-permute-start.20 = (f32[8,512]{1,0:T(8,128)S(1)}, f32[8,512]{1,0:T(8,128)S(1)}, u32[]{:S(2)}, u32[]{:S(2)}) collective-permute-start(f32[8,512]{1,0:T(8,128)S(1)} %get-tuple-element.94), channel_id=1, source_target_pairs={{26,24},{28,30}} | collective-permute-start | bytes 49160 | tf_op jit(solution)/shard_map/ppermute | solution.py:630
  (6 other events, 52.4 us)

commit v2 on v1

--- a/solution.py
+++ b/solution.py
@@ -201,8 +201,8 @@
     count = chunk.shape[0] // z.buf
     span = count * z.part
 
-    def kernel(by_rows, got, own_hi, own_lo, own_tail, *rest):
-        outs, (left, right) = rest[:count], rest[count:]
+    def kernel(by_rows, got, own_hi, own_lo, own_tail, res_out, left, right):
+        outs = split_parts(z, [res_out])
         gots = split_parts(z, [got])
 
         @pl.when(by_rows)
@@ -232,7 +232,7 @@
 
     return call(
         kernel,
-        [shape(z.buf, z.part)] * count,
+        [shape(count * z.buf, z.part)],
         [chunk, *own],
         where,
         scratch=[pltpu.VMEM((span + z.low, z.width), F32), pltpu.VMEM((z.width + z.series, span), F32)],
@@ -396,10 +396,10 @@
 
             @pl.when(swap)
             def _():
-                if len(rest) == 1:
+                if rest[0].shape[0] == z.tall:
                     full[...] = rest[0][...]
                 else:
-                    gather(z, by_rows, rest, full)
+                    gather(z, by_rows, split_parts(z, rest), full)
 
         hi[...], lo[...] = halves(full[...])
         if with_tail:
@@ -446,17 +446,21 @@
     return res if split else res[0]
 
 
-def pick(where, one, two):
-    def kernel(flag, a, b, out):
+def pick_halves(where, whole, parts):
+    rows = parts[0].shape[0]
+
+    def kernel(flag, a, b, c, first, second):
         @pl.when(flag)
         def _():
-            out[...] = a[...]
+            first[...] = a[:rows]
+            second[...] = a[rows:]
 
         @pl.when(jnp.logical_not(flag))
         def _():
-            out[...] = b[...]
-
-    return call(kernel, shape(*one.shape), [one, two], where)
+            first[...] = b[...]
+            second[...] = c[...]
+
+    return call(kernel, [shape(*p.shape) for p in parts], [whole, *parts], where)
 
 
 def advance_mean(z, mean, block):
@@ -503,6 +507,9 @@
     maps = list(left) + ([] if cross is None else list(cross))
 
     def kernel(flag, *refs):
+        pl.when((flag[0] >= 0) & (flag[0] < m))(lambda: run(flag, *refs))
+
+    def run(flag, *refs):
         index, through, in_right = flag
         hi, lo, tail = refs[m : m + 3]
         mine, other, now = refs[m + len(maps) :]
@@ -704,16 +711,17 @@
         nexts = [(b, size + r) for r in tree.child_roots(1, depth, 0)]
         second = send(onward, nexts[1:]) + send(onward, nexts[:1])
         roots = tree.pairs(lambda odd: [(r, r ^ 1) for r in tree.child_roots(odd, depth, 0)])
-        roots = [p for p in roots if p[0] >= size]
-        got = [send(c, roots) for c in final]
+        got = [send(c, [p for p in roots if p[0] // size == 1]) for c in final]
+        rest = [send(c, [p for p in roots if p[0] // size > 1]) for c in final]
         left = assemble(z, lambda seg, tm: (seg >= 0, seg % 2 == 1), first, [back])
         halfway = assemble(z, lambda seg, tm: (seg >= 0, seg < 0), crossed)
-        got[-1], left, halfway = lax.optimization_barrier((got[-1], left, halfway))
+        rest[-1], left, halfway = lax.optimization_barrier((rest[-1], left, halfway))
 
         def beside(seg, tm):
             return tm >= half, tm ^ 1 == tree.root_of(seg % 2, depth - 1, tm // half)
 
         block = assemble(z, beside, final, got, with_tail=False)
+        later = assemble(z, beside, final, rest, with_tail=False)
 
         at_root = assemble(z, lambda seg, tm: (tm >= half, seg < 0), final)
         entries = [init_mean, second]
@@ -727,11 +735,8 @@
 
         same, aside = advance(z, lambda seg, tm: seg == 0, start, at_root, split=True)
         first_roots = tree.child_roots(0, depth, 0)
-        moved = pick(
-            lambda seg, tm: tm == tree.root_of(0, depth - 1, tm // half),
-            same,
-            send(aside, [(r, r ^ 1) for r in first_roots]),
-        )
+        beside_first = send(aside, [(r, r ^ 1) for r in first_roots])
+        moved = same
         for turn in range(1, segs):
             pairs = [((turn - 1) * size + i, turn * size + i) for i in range(size) if tree.holds(i)]
             if turn == 1:
@@ -743,7 +748,7 @@
             def where(seg, tm, turn=turn):
                 return seg >= turn
 
-            moved = advance(z, where, [arrived], block, moved, turn == segs - 1)
+            moved = advance(z, where, [arrived], block if turn == 1 else later, moved, turn == segs - 1)
 
         def down(arrivals, first_seg, last_seg):
             def only(pairs):
@@ -766,7 +771,9 @@
 
         candidates = down(entries[:-1], 0, segs - 2) + down(entries[-1:], segs - 1, segs - 1)
 
-        kept, given = moved
+        kept, given = pick_halves(
+            lambda seg, tm: (seg == 0) & (tm == tree.root_of(0, depth - 1, tm // half) ^ 1), beside_first, moved
+        )
         for bit in reversed(bits):
             back_pairs = [(b, a) for a, b in tree.far(bit)]
             came = send(given, back_pairs)

time: 97.8 us -> 94.5 us (0.966)
  the two profiles are of different devices: /device:TPU:5 before, /device:TPU:15 now
where the time goes in v2:
time: 94.5 us; the launch traced here: 93.8 us
  waiting for transfers between devices  48.7 us (52%)
  starting transfers between devices  30 us (32%)
  Pallas kernels  13.7 us (14%)
  between operations  1.33 us (1%)
    ppermute x35, waiting for transfers between devices, send(): return lax.ppermute(x, AXES, pairs)  48.7 us
    ppermute x35, starting transfers between devices, send(): return lax.ppermute(x, AXES, pairs)  30 us
    pallas_call x28, Pallas kernels, call(): pl.pallas_call(body, out_shape=outs, in_specs=in_specs, out_specs=jax.tre...  13.7 us
  transfers between devices with their start and end apart: 35, of which 8 were waited for; matrix products, arithmetic and copies ran while one was open for 0% of the time, Pallas kernels for 10%

profile of v2, /device:TPU:15, one launch (start us, length us, event | category | flops | bytes accessed | tf_op | source)
XLA Modules:
  0.0 93.8 jit_solution(4831966905036289858)
XLA Ops:
  0.6 2.2 %shard_map.68 = (f32[528,128]{1,0:T(8,128)S(1)}, f32[528,128]{1,0:T(8,128)S(1)}, f32[528,128]{1,0:T(8,128)S(1)}, f32[528,128]{1,0:T(8,128)S(1)}, f32[2,4,512]{2,1,0:T(4,128)S(1)}) custom-call(bf16[2,512,512]{2,1,0:T(8,128)(2,1)} %refs_11_.1, bf16[2,512,512]{2,1,0:T(8,128)(2,1)} %refs_1_.3, bf16[2,4,512]{2,1,0:T(4,128)(2,1)} %refs_2_.3), custom_call_target="tpu_custom_call" | custom-call | tf_op jit(solution)/shard_map/pallas_call | solution.py:101
  2.8 1.3 %collective-permute-start = (f32[528,128]{1,0:T(8,128)S(1)}, f32[528,128]{1,0:T(8,128)S(1)}, u32[]{:S(2)}, u32[]{:S(2)}) collective-permute-start(f32[528,128]{1,0:T(8,128)S(1)} %get-tuple-element.55), channel_id=1, source_target_pairs={{0,1},{2,3},{4,5},{6,7},{9,8},{11,10},{13,12},{15,14},{16,17},{18,... | collective-permute-start | bytes 811016 | tf_op jit(solution)/shard_map/ppermute | solution.py:637
  4.1 1.3 %collective-permute-start.2 = (f32[528,128]{1,0:T(8,128)S(1)}, f32[528,128]{1,0:T(8,128)S(1)}, u32[]{:S(2)}, u32[]{:S(2)}) collective-permute-start(f32[528,128]{1,0:T(8,128)S(1)} %get-tuple-element.59), channel_id=1, source_target_pairs={{0,1},{2,3},{4,5},{6,7},{9,8},{11,10},{13,12},{15,14},{16,17},{18,... | collective-permute-start | bytes 811016 | tf_op jit(solution)/shard_map/ppermute | solution.py:637
  5.5 1.3 %collective-permute-start.4 = (f32[528,128]{1,0:T(8,128)S(1)}, f32[528,128]{1,0:T(8,128)S(1)}, u32[]{:S(2)}, u32[]{:S(2)}) collective-permute-start(f32[528,128]{1,0:T(8,128)S(1)} %get-tuple-element.60), channel_id=1, source_target_pairs={{0,1},{2,3},{4,5},{6,7},{9,8},{11,10},{13,12},{15,14},{16,17},{18,... | collective-permute-start | bytes 811016 | tf_op jit(solution)/shard_map/ppermute | solution.py:637
  6.8 1.3 %collective-permute-start.6 = (f32[528,128]{1,0:T(8,128)S(1)}, f32[528,128]{1,0:T(8,128)S(1)}, u32[]{:S(2)}, u32[]{:S(2)}) collective-permute-start(f32[528,128]{1,0:T(8,128)S(1)} %get-tuple-element.61), channel_id=1, source_target_pairs={{0,1},{2,3},{4,5},{6,7},{9,8},{11,10},{13,12},{15,14},{16,17},{18,... | collective-permute-start | bytes 811016 | tf_op jit(solution)/shard_map/ppermute | solution.py:637
  8.8 0.7 collective-permute-start.1
  9.5 1.0 %collective-permute-done.2.refs_0_.refs_1_ = f32[528,128]{1,0:T(8,128)S(1)} collective-permute-done((f32[528,128]{1,0:T(8,128)S(1)}, f32[528,128]{1,0:T(8,128)S(1)}, u32[]{:S(2)}, u32[]{:S(2)}) %collective-permute-start.2) | collective-permute-done | bytes 270368 | tf_op jit(solution)/shard_map/ppermute | solution.py:637
  11.0 0.7 collective-permute-start.3
  11.7 1.6 %collective-permute-done.4.refs_0_.refs_2_ = f32[528,128]{1,0:T(8,128)S(1)} collective-permute-done((f32[528,128]{1,0:T(8,128)S(1)}, f32[528,128]{1,0:T(8,128)S(1)}, u32[]{:S(2)}, u32[]{:S(2)}) %collective-permute-start.4) | collective-permute-done | bytes 270368 | tf_op jit(solution)/shard_map/ppermute | solution.py:637
  13.9 0.7 collective-permute-start.5
  14.6 1.6 %collective-permute-done.6.refs_0_.refs_3_ = f32[528,128]{1,0:T(8,128)S(1)} collective-permute-done((f32[528,128]{1,0:T(8,128)S(1)}, f32[528,128]{1,0:T(8,128)S(1)}, u32[]{:S(2)}, u32[]{:S(2)}) %collective-permute-start.6) | collective-permute-done | bytes 270368 | tf_op jit(solution)/shard_map/ppermute | solution.py:637
  16.8 0.7 collective-permute-start.7
  17.5 1.2 %shard_map.74 = (f32[1056,128]{1,0:T(8,128)S(1)}, bf16[528,512]{1,0:T(8,128)(2,1)S(1)}, bf16[528,512]{1,0:T(8,128)(2,1)S(1)}, f32[4,512]{1,0:T(4,128)S(1)}, bf16...) custom-call(f32[528,128]{1,0:T(8,128)S(1)} %collective-permute-done.1.refs_0_, ...), custom_call_target="tpu_custom_call" | custom-call | tf_op jit(solution)/shard_map/pallas_call | solution.py:101
  18.7 0.7 collective-permute-start.11
  19.5 0.8 shard_map.75
  20.3 0.7 collective-permute-start.12
  21.0 1.3 %collective-permute-start.15 = (f32[528,512]{1,0:T(8,128)S(1)}, f32[528,512]{1,0:T(8,128)S(1)}, u32[]{:S(2)}, u32[]{:S(2)}) collective-permute-start(f32[528,512]{1,0:T(8,128)S(1)} %get-tuple-element.77), channel_id=1, source_target_pairs={{8,9},{10,11},{12,13},{14,15},{24,25},{26,27},{28,29},{30,31}} | collective-permute-start | bytes 3244040 | tf_op jit(solution)/shard_map/ppermute | solution.py:637
  26.6 0.7 collective-permute-start.29
  27.3 0.7 collective-permute-start.30
  28.7 1.3 %collective-permute-start.14 = (f32[1056,128]{1,0:T(8,128)S(1)}, f32[1056,128]{1,0:T(8,128)S(1)}, u32[]{:S(2)}, u32[]{:S(2)}) collective-permute-start(f32[1056,128]{1,0:T(8,128)S(1)} %shard_map.79.refs_1_), channel_id=1, source_target_pairs={{19,18},{21,20},{26,27},{28,29}} | collective-permute-start | bytes 1622024 | tf_op jit(solution)/shard_map/ppermute | solution.py:637
  30.0 1.3 %collective-permute-start.32 = (f32[1056,128]{1,0:T(8,128)S(1)}, f32[1056,128]{1,0:T(8,128)S(1)}, u32[]{:S(2)}, u32[]{:S(2)}) collective-permute-start(f32[1056,128]{1,0:T(8,128)S(1)} %shard_map.78.refs_0_), channel_id=1, source_target_pairs={{19,18},{21,20},{26,27},{28,29}} | collective-permute-start | bytes 1622024 | tf_op jit(solution)/shard_map/ppermute | solution.py:637
  33.2 13.8 %collective-permute-done.15.refs_4_ = f32[528,512]{1,0:T(8,128)S(1)} collective-permute-done((f32[528,512]{1,0:T(8,128)S(1)}, f32[528,512]{1,0:T(8,128)S(1)}, u32[]{:S(2)}, u32[]{:S(2)}) %collective-permute-start.15) | collective-permute-done | bytes 1081376 | tf_op jit(solution)/shard_map/ppermute | solution.py:637
  47.3 7.5 %collective-permute-done.14.refs_3_ = f32[1056,128]{1,0:T(8,128)S(1)} collective-permute-done((f32[1056,128]{1,0:T(8,128)S(1)}, f32[1056,128]{1,0:T(8,128)S(1)}, u32[]{:S(2)}, u32[]{:S(2)}) %collective-permute-start.14) | collective-permute-done | bytes 540704 | tf_op jit(solution)/shard_map/ppermute | solution.py:637
  54.8 5.8 %collective-permute-done.32.refs_2_ = f32[1056,128]{1,0:T(8,128)S(1)} collective-permute-done((f32[1056,128]{1,0:T(8,128)S(1)}, f32[1056,128]{1,0:T(8,128)S(1)}, u32[]{:S(2)}, u32[]{:S(2)}) %collective-permute-start.32) | collective-permute-done | bytes 540704 | tf_op jit(solution)/shard_map/ppermute | solution.py:637
  61.3 1.3 %collective-permute-start.33 = (f32[128,512]{1,0:T(8,128)S(1)}, f32[128,512]{1,0:T(8,128)S(1)}, u32[]{:S(2)}, u32[]{:S(2)}) collective-permute-start(f32[128,512]{1,0:T(8,128)S(1)} %shard_map.92.refs_3_), channel_id=1, source_target_pairs={{18,26},{19,27},{20,28},{21,29}} | collective-permute-start | bytes 786440 | tf_op jit(solution)/shard_map/ppermute | solution.py:637
  62.6 0.7 collective-permute-start.26
  63.3 7.5 %collective-permute-done.33.refs_0_ = f32[128,512]{1,0:T(8,128)S(1)} collective-permute-done((f32[128,512]{1,0:T(8,128)S(1)}, f32[128,512]{1,0:T(8,128)S(1)}, u32[]{:S(2)}, u32[]{:S(2)}) %collective-permute-start.33) | collective-permute-done | bytes 262176 | tf_op jit(solution)/shard_map/ppermute | solution.py:637
  71.2 1.3 %collective-permute-start.34 = (f32[64,512]{1,0:T(8,128)S(1)}, f32[64,512]{1,0:T(8,128)S(1)}, u32[]{:S(2)}, u32[]{:S(2)}) collective-permute-start(f32[64,512]{1,0:T(8,128)S(1)} %get-tuple-element.107), channel_id=1, source_target_pairs={{2,0},{3,1},{4,6},{5,7},{10,8},{11,9},{12,14},{13,15},{18,16},{19,... | collective-permute-start | bytes 393224 | tf_op jit(solution)/shard_map/ppermute | solution.py:637
  77.0 0.8 collective-permute-start.16
  80.8 1.3 %collective-permute-start.22 = (f32[8,512]{1,0:T(8,128)S(1)}, f32[8,512]{1,0:T(8,128)S(1)}, u32[]{:S(2)}, u32[]{:S(2)}) collective-permute-start(f32[8,512]{1,0:T(8,128)S(1)} %get-tuple-element.89.refs_4_), channel_id=1, source_target_pairs={{26,27},{28,29}} | collective-permute-start | bytes 49160 | tf_op jit(solution)/shard_map/ppermute | solution.py:637
  82.1 9.8 %collective-permute-done.22.refs_7_ = f32[8,512]{1,0:T(8,128)S(1)} collective-permute-done((f32[8,512]{1,0:T(8,128)S(1)}, f32[8,512]{1,0:T(8,128)S(1)}, u32[]{:S(2)}, u32[]{:S(2)}) %collective-permute-start.22) | collective-permute-done | bytes 16416 | tf_op jit(solution)/shard_map/ppermute | solution.py:637
  91.9 1.2 %shard_map.87 = f32[2,4,512]{2,1,0:T(4,128)} custom-call(f32[8,512]{1,0:T(8,128)S(1)} %get-tuple-element.87.refs_0_, f32[8,512]{1,0:T(8,128)S(1)} %collective-permute-done.16.refs_1_, f32[8,512]{1,0:T(8,128)S(1)} %collective-permute-done.17.refs_2_, f32[8,512]{1,0:T(8,128)S(1)} %collective-permute-done.18.refs_3_, f32[8,512]{1,0:T(8,128)S(1)} %get-tuple-element.89.refs_4_, ...), custom_call_target="tpu_custom_call" | custom-call | tf_op jit(solution)/shard_map/pallas_call | solution.py:101
  (74 shorter events, 18.5 us)
Async XLA Ops:
  2.8 5.3 %collective-permute-start = (f32[528,128]{1,0:T(8,128)S(1)}, f32[528,128]{1,0:T(8,128)S(1)}, u32[]{:S(2)}, u32[]{:S(2)}) collective-permute-start(f32[528,128]{1,0:T(8,128)S(1)} %get-tuple-element.55), channel_id=1, source_target_pairs={{0,1},{2,3},{4,5},{6,7},{9,8},{11,10},{13,12},{15,14},{16,17},{18,... | collective-permute-start | bytes 811016 | tf_op jit(solution)/shard_map/ppermute | solution.py:637
  4.1 6.3 %collective-permute-start.2 = (f32[528,128]{1,0:T(8,128)S(1)}, f32[528,128]{1,0:T(8,128)S(1)}, u32[]{:S(2)}, u32[]{:S(2)}) collective-permute-start(f32[528,128]{1,0:T(8,128)S(1)} %get-tuple-element.59), channel_id=1, source_target_pairs={{0,1},{2,3},{4,5},{6,7},{9,8},{11,10},{13,12},{15,14},{16,17},{18,... | collective-permute-start | bytes 811016 | tf_op jit(solution)/shard_map/ppermute | solution.py:637
  5.5 7.8 %collective-permute-start.4 = (f32[528,128]{1,0:T(8,128)S(1)}, f32[528,128]{1,0:T(8,128)S(1)}, u32[]{:S(2)}, u32[]{:S(2)}) collective-permute-start(f32[528,128]{1,0:T(8,128)S(1)} %get-tuple-element.60), channel_id=1, source_target_pairs={{0,1},{2,3},{4,5},{6,7},{9,8},{11,10},{13,12},{15,14},{16,17},{18,... | collective-permute-start | bytes 811016 | tf_op jit(solution)/shard_map/ppermute | solution.py:637
  6.8 9.4 %collective-permute-start.6 = (f32[528,128]{1,0:T(8,128)S(1)}, f32[528,128]{1,0:T(8,128)S(1)}, u32[]{:S(2)}, u32[]{:S(2)}) collective-permute-start(f32[528,128]{1,0:T(8,128)S(1)} %get-tuple-element.61), channel_id=1, source_target_pairs={{0,1},{2,3},{4,5},{6,7},{9,8},{11,10},{13,12},{15,14},{16,17},{18,... | collective-permute-start | bytes 811016 | tf_op jit(solution)/shard_map/ppermute | solution.py:637
  8.8 8.7 %collective-permute-start.1 = (f32[528,128]{1,0:T(8,128)S(1)}, f32[528,128]{1,0:T(8,128)S(1)}, u32[]{:S(2)}, u32[]{:S(2)}) collective-permute-start(f32[528,128]{1,0:T(8,128)S(1)} %shard_map.70.refs_4_), channel_id=1, source_target_pairs={{1,3},{7,5},{8,10},{14,12},{17,19},{23,21},{24,26},{30,28}} | collective-permute-start | bytes 811016 | tf_op jit(solution)/shard_map/ppermute | solution.py:637
  11.0 6.5 %collective-permute-start.3 = (f32[528,128]{1,0:T(8,128)S(1)}, f32[528,128]{1,0:T(8,128)S(1)}, u32[]{:S(2)}, u32[]{:S(2)}) collective-permute-start(f32[528,128]{1,0:T(8,128)S(1)} %shard_map.71.refs_5_), channel_id=1, source_target_pairs={{1,3},{7,5},{8,10},{14,12},{17,19},{23,21},{24,26},{30,28}} | collective-permute-start | bytes 811016 | tf_op jit(solution)/shard_map/ppermute | solution.py:637
  13.9 3.6 %collective-permute-start.5 = (f32[528,128]{1,0:T(8,128)S(1)}, f32[528,128]{1,0:T(8,128)S(1)}, u32[]{:S(2)}, u32[]{:S(2)}) collective-permute-start(f32[528,128]{1,0:T(8,128)S(1)} %shard_map.72.refs_6_), channel_id=1, source_target_pairs={{1,3},{7,5},{8,10},{14,12},{17,19},{23,21},{24,26},{30,28}} | collective-permute-start | bytes 811016 | tf_op jit(solution)/shard_map/ppermute | solution.py:637
  16.8 0.7 collective-permute-start.7
  18.7 4.9 %collective-permute-start.11 = (f32[1056,128]{1,0:T(8,128)S(1)}, f32[1056,128]{1,0:T(8,128)S(1)}, u32[]{:S(2)}, u32[]{:S(2)}) collective-permute-start(f32[1056,128]{1,0:T(8,128)S(1)} %get-tuple-element.62.refs_0_), channel_id=1, source_target_pairs={{3,5},{5,3},{10,12},{12,10},{19,21},{21,19},{26,28},{28,26}} | collective-permute-start | bytes 1622024 | tf_op jit(solution)/shard_map/ppermute | solution.py:637
  20.3 4.7 %collective-permute-start.12 = (f32[1056,128]{1,0:T(8,128)S(1)}, f32[1056,128]{1,0:T(8,128)S(1)}, u32[]{:S(2)}, u32[]{:S(2)}) collective-permute-start(f32[1056,128]{1,0:T(8,128)S(1)} %get-tuple-element.72), channel_id=1, source_target_pairs={{3,5},{5,3},{10,12},{12,10},{19,21},{21,19},{26,28},{28,26}} | collective-permute-start | bytes 1622024 | tf_op jit(solution)/shard_map/ppermute | solution.py:637
  21.0 26.1 %collective-permute-start.15 = (f32[528,512]{1,0:T(8,128)S(1)}, f32[528,512]{1,0:T(8,128)S(1)}, u32[]{:S(2)}, u32[]{:S(2)}) collective-permute-start(f32[528,512]{1,0:T(8,128)S(1)} %get-tuple-element.77), channel_id=1, source_target_pairs={{8,9},{10,11},{12,13},{14,15},{24,25},{26,27},{28,29},{30,31}} | collective-permute-start | bytes 3244040 | tf_op jit(solution)/shard_map/ppermute | solution.py:637
  22.3 3.6 %collective-permute-start.23 = (f32[64,512]{1,0:T(8,128)S(1)}, f32[64,512]{1,0:T(8,128)S(1)}, u32[]{:S(2)}, u32[]{:S(2)}) collective-permute-start(f32[64,512]{1,0:T(8,128)S(1)} %copy-done.1), channel_id=1, source_target_pairs={{1,3},{7,5}} | collective-permute-start | bytes 393224 | tf_op jit(solution)/shard_map/ppermute | solution.py:637
  23.0 2.9 %collective-permute-start.24 = (f32[64,512]{1,0:T(8,128)S(1)}, f32[64,512]{1,0:T(8,128)S(1)}, u32[]{:S(2)}, u32[]{:S(2)}) collective-permute-start(f32[64,512]{1,0:T(8,128)S(1)} %copy-done.1), channel_id=1, source_target_pairs={{2,3},{4,5}} | collective-permute-start | bytes 393224 | tf_op jit(solution)/shard_map/ppermute | solution.py:637
  23.6 2.3 %collective-permute-start.25 = (f32[64,512]{1,0:T(8,128)S(1)}, f32[64,512]{1,0:T(8,128)S(1)}, u32[]{:S(2)}, u32[]{:S(2)}) collective-permute-start(f32[64,512]{1,0:T(8,128)S(1)} %copy-done.1), channel_id=1, source_target_pairs={{0,3},{6,5}} | collective-permute-start | bytes 393224 | tf_op jit(solution)/shard_map/ppermute | solution.py:637
  25.9 2.8 %collective-permute-start.27 = (f32[128,512]{1,0:T(8,128)S(1)}, f32[128,512]{1,0:T(8,128)S(1)}, u32[]{:S(2)}, u32[]{:S(2)}) collective-permute-start(f32[128,512]{1,0:T(8,128)S(1)} %get-tuple-element.98.refs_3_), channel_id=1, source_target_pairs={{3,11},{5,13}} | collective-permute-start | bytes 786440 | tf_op jit(solution)/shard_map/ppermute | solution.py:637
  26.6 4.8 %collective-permute-start.29 = (f32[1056,128]{1,0:T(8,128)S(1)}, f32[1056,128]{1,0:T(8,128)S(1)}, u32[]{:S(2)}, u32[]{:S(2)}) collective-permute-start(f32[1056,128]{1,0:T(8,128)S(1)} %shard_map.78.refs_0_), channel_id=1, source_target_pairs={{10,11},{12,13}} | collective-permute-start | bytes 1622024 | tf_op jit(solution)/shard_map/ppermute | solution.py:637
  27.3 4.1 %collective-permute-start.30 = (f32[1056,128]{1,0:T(8,128)S(1)}, f32[1056,128]{1,0:T(8,128)S(1)}, u32[]{:S(2)}, u32[]{:S(2)}) collective-permute-start(f32[1056,128]{1,0:T(8,128)S(1)} %shard_map.79.refs_1_), channel_id=1, source_target_pairs={{10,11},{12,13}} | collective-permute-start | bytes 1622024 | tf_op jit(solution)/shard_map/ppermute | solution.py:637
  28.0 2.0 %collective-permute-start.28 = (f32[128,512]{1,0:T(8,128)S(1)}, f32[128,512]{1,0:T(8,128)S(1)}, u32[]{:S(2)}, u32[]{:S(2)}) collective-permute-start(f32[128,512]{1,0:T(8,128)S(1)} %get-tuple-element.97), channel_id=1, source_target_pairs={{3,10},{5,12}} | collective-permute-start | bytes 786440 | tf_op jit(solution)/shard_map/ppermute | solution.py:637
  28.7 26.1 %collective-permute-start.14 = (f32[1056,128]{1,0:T(8,128)S(1)}, f32[1056,128]{1,0:T(8,128)S(1)}, u32[]{:S(2)}, u32[]{:S(2)}) collective-permute-start(f32[1056,128]{1,0:T(8,128)S(1)} %shard_map.79.refs_1_), channel_id=1, source_target_pairs={{19,18},{21,20},{26,27},{28,29}} | collective-permute-start | bytes 1622024 | tf_op jit(solution)/shard_map/ppermute | solution.py:637
  30.0 30.5 %collective-permute-start.32 = (f32[1056,128]{1,0:T(8,128)S(1)}, f32[1056,128]{1,0:T(8,128)S(1)}, u32[]{:S(2)}, u32[]{:S(2)}) collective-permute-start(f32[1056,128]{1,0:T(8,128)S(1)} %shard_map.78.refs_0_), channel_id=1, source_target_pairs={{19,18},{21,20},{26,27},{28,29}} | collective-permute-start | bytes 1622024 | tf_op jit(solution)/shard_map/ppermute | solution.py:637
  32.1 28.8 %collective-permute-start.31 = (f32[128,512]{1,0:T(8,128)S(1)}, f32[128,512]{1,0:T(8,128)S(1)}, u32[]{:S(2)}, u32[]{:S(2)}) collective-permute-start(f32[128,512]{1,0:T(8,128)S(1)} %shard_map.90.refs_3_), channel_id=1, source_target_pairs={{10,18},{11,19},{12,20},{13,21}} | collective-permute-start | bytes 786440 | tf_op jit(solution)/shard_map/ppermute | solution.py:637
  61.3 9.5 %collective-permute-start.33 = (f32[128,512]{1,0:T(8,128)S(1)}, f32[128,512]{1,0:T(8,128)S(1)}, u32[]{:S(2)}, u32[]{:S(2)}) collective-permute-start(f32[128,512]{1,0:T(8,128)S(1)} %shard_map.92.refs_3_), channel_id=1, source_target_pairs={{18,26},{19,27},{20,28},{21,29}} | collective-permute-start | bytes 786440 | tf_op jit(solution)/shard_map/ppermute | solution.py:637
  62.6 8.6 %collective-permute-start.26 = (f32[128,512]{1,0:T(8,128)S(1)}, f32[128,512]{1,0:T(8,128)S(1)}, u32[]{:S(2)}, u32[]{:S(2)}) collective-permute-start(f32[128,512]{1,0:T(8,128)S(1)} %get-tuple-element.97), channel_id=1, source_target_pairs={{3,2},{5,4}} | collective-permute-start | bytes 786440 | tf_op jit(solution)/shard_map/ppermute | solution.py:637
  71.2 22.0 %collective-permute-start.34 = (f32[64,512]{1,0:T(8,128)S(1)}, f32[64,512]{1,0:T(8,128)S(1)}, u32[]{:S(2)}, u32[]{:S(2)}) collective-permute-start(f32[64,512]{1,0:T(8,128)S(1)} %get-tuple-element.107), channel_id=1, source_target_pairs={{2,0},{3,1},{4,6},{5,7},{10,8},{11,9},{12,14},{13,15},{18,16},{19,... | collective-permute-start | bytes 393224 | tf_op jit(solution)/shard_map/ppermute | solution.py:637
  73.7 1.3 %collective-permute-start.9 = (f32[8,512]{1,0:T(8,128)S(1)}, f32[8,512]{1,0:T(8,128)S(1)}, u32[]{:S(2)}, u32[]{:S(2)}) collective-permute-start(f32[8,512]{1,0:T(8,128)S(1)} %shard_map.77), channel_id=1, source_target_pairs={{5,12}} | collective-permute-start | bytes 49160 | tf_op jit(solution)/shard_map/ppermute | solution.py:637
  76.3 2.2 %collective-permute-start.19 = (f32[8,512]{1,0:T(8,128)S(1)}, f32[8,512]{1,0:T(8,128)S(1)}, u32[]{:S(2)}, u32[]{:S(2)}) collective-permute-start(f32[8,512]{1,0:T(8,128)S(1)} %shard_map.85), channel_id=1, source_target_pairs={{19,26},{21,28}} | collective-permute-start | bytes 49160 | tf_op jit(solution)/shard_map/ppermute | solution.py:637
  77.0 3.1 %collective-permute-start.16 = (f32[8,512]{1,0:T(8,128)S(1)}, f32[8,512]{1,0:T(8,128)S(1)}, u32[]{:S(2)}, u32[]{:S(2)}) collective-permute-start(f32[8,512]{1,0:T(8,128)S(1)} %get-tuple-element.88), channel_id=1, source_target_pairs={{3,1},{5,7},{10,8},{12,14},{19,17},{21,23}} | collective-permute-start | bytes 49160 | tf_op jit(solution)/shard_map/ppermute | solution.py:637
  77.8 3.0 %collective-permute-start.17 = (f32[8,512]{1,0:T(8,128)S(1)}, f32[8,512]{1,0:T(8,128)S(1)}, u32[]{:S(2)}, u32[]{:S(2)}) collective-permute-start(f32[8,512]{1,0:T(8,128)S(1)} %get-tuple-element.88), channel_id=1, source_target_pairs={{3,0},{5,6},{10,9},{12,15},{19,16},{21,22}} | collective-permute-start | bytes 49160 | tf_op jit(solution)/shard_map/ppermute | solution.py:637
  78.7 3.3 %collective-permute-start.20 = (f32[8,512]{1,0:T(8,128)S(1)}, f32[8,512]{1,0:T(8,128)S(1)}, u32[]{:S(2)}, u32[]{:S(2)}) collective-permute-start(f32[8,512]{1,0:T(8,128)S(1)} %get-tuple-element.90), channel_id=1, source_target_pairs={{26,24},{28,30}} | collective-permute-start | bytes 49160 | tf_op jit(solution)/shard_map/ppermute | solution.py:637
  79.4 2.7 %collective-permute-start.21 = (f32[8,512]{1,0:T(8,128)S(1)}, f32[8,512]{1,0:T(8,128)S(1)}, u32[]{:S(2)}, u32[]{:S(2)}) collective-permute-start(f32[8,512]{1,0:T(8,128)S(1)} %get-tuple-element.90), channel_id=1, source_target_pairs={{26,25},{28,31}} | collective-permute-start | bytes 49160 | tf_op jit(solution)/shard_map/ppermute | solution.py:637
  80.1 2.0 %collective-permute-start.18 = (f32[8,512]{1,0:T(8,128)S(1)}, f32[8,512]{1,0:T(8,128)S(1)}, u32[]{:S(2)}, u32[]{:S(2)}) collective-permute-start(f32[8,512]{1,0:T(8,128)S(1)} %get-tuple-element.87.refs_0_), channel_id=1, source_target_pairs={{3,2},{5,4},{10,11},{12,13},{19,18},{21,20}} | collective-permute-start | bytes 49160 | tf_op jit(solution)/shard_map/ppermute | solution.py:637
  80.8 11.2 %collective-permute-start.22 = (f32[8,512]{1,0:T(8,128)S(1)}, f32[8,512]{1,0:T(8,128)S(1)}, u32[]{:S(2)}, u32[]{:S(2)}) collective-permute-start(f32[8,512]{1,0:T(8,128)S(1)} %get-tuple-element.89.refs_4_), channel_id=1, source_target_pairs={{26,27},{28,29}} | collective-permute-start | bytes 49160 | tf_op jit(solution)/shard_map/ppermute | solution.py:637
  (6 other events, 31.1 us)
